TPU v7x, 32 devices: a whole 2x2x4 slice. The times are simulated.
32 devices in a mesh: fsdp: 8 (over z, core), rows: 4 (over y, x).
Axes of the slice: x: 2, y: 2, z: 4, core: 2. Of those that a mesh axis runs over, the one named last changes fastest.
Arguments:
- query_rows: bfloat16 [8, 1024, 1536], P('fsdp', 'rows'), may hold values from -6 to 6
- key_rows: bfloat16 [8, 1024, 1536], P('fsdp', 'rows'), may hold values from -6 to 6
- value_rows: bfloat16 [8, 1024, 1536], P('fsdp', 'rows'), may hold values from -6 to 6
- grad_out: bfloat16 [8, 1024, 3072], P('fsdp', 'rows'), may hold values from -6 to 6
- w_out: bfloat16 [1536, 3072], P('fsdp'), may hold values from -0.15625 to 0.15625
Outputs:
- grad_query: bfloat16 [8, 1024, 1536], P('fsdp', 'rows')
- grad_key: bfloat16 [8, 1024, 1536], P('fsdp', 'rows')
- grad_value: bfloat16 [8, 1024, 1536], P('fsdp', 'rows')
- grad_w_out: float32 [1536, 3072], P('fsdp')
All inputs are finite; a program needn't handle non-finite values.
Results may differ from a plain program's by a relative error of at most 0.02.
Values may be sent and summed in bfloat16 or wider, within the bound.
No kernel may reach another device: no remote copies, remote signals or barrier semaphores. Data moves between devices by JAX's collectives and lax.ppermute only.
A program may use at most 192 MiB of HBM per device.

v0:
```python
import functools
import math

import jax
import jax.numpy as jnp
from jax import lax
from jax.experimental import pallas as pl
from jax.experimental.pallas import tpu as pltpu
from jax.sharding import PartitionSpec as P


HDIM = 128


NT = (((1,), (1,)), ((), ()))
NN = (((1,), (0,)), ((), ()))


def dot(a, b, dims=NN):
    return lax.dot_general(a, b, dims, preferred_element_type=jnp.float32)


def whole(shape):
    return pl.BlockSpec(shape, lambda *_: (0,) * len(shape))


def cost(flops, moved, exps=0):
    return pl.CostEstimate(flops=flops, bytes_accessed=moved, transcendentals=exps)


def pack(place, query, key, value, rows):
    tokens, width = query.shape[1], query.shape[2] // rows

    def body(place_ref, *refs):
        ins, outs, (held, sems) = refs[:3], refs[3:-2], refs[-2:]
        moves = []
        for slot in (*range(1, rows), 0):
            start = pl.multiple_of((place_ref[0] ^ slot) * width, HDIM)
            for at in range(3):
                box = held.at[slot, at]
                moves.append(
                    (
                        pltpu.make_async_copy(
                            ins[at].at[0, :, pl.ds(start, width)], box, sems.at[0, slot, at]
                        ),
                        pltpu.make_async_copy(box, outs[slot].at[at], sems.at[1, slot, at]),
                    )
                )
        run(moves)

    shape = (3, tokens, width)
    return pl.pallas_call(
        body,
        grid_spec=pltpu.PrefetchScalarGridSpec(
            num_scalar_prefetch=1,
            grid=(1,),
            in_specs=[pl.BlockSpec(memory_space=pltpu.HBM)] * 3,
            out_specs=[pl.BlockSpec(memory_space=pltpu.HBM)] * rows,
            scratch_shapes=[
                pltpu.VMEM((rows, *shape), query.dtype),
                pltpu.SemaphoreType.DMA((2, rows, 3)),
            ],
        ),
        out_shape=[jax.ShapeDtypeStruct(shape, query.dtype)] * rows,
        cost_estimate=cost(0, 12 * query.size),
        name="pack",
    )(place, query, key, value)


def run(moves, rest=None):
    for fetch, _ in moves:
        fetch.start()
    for fetch, store in moves:
        fetch.wait()
        store.start()
    for store in rest() if rest else ():
        store.wait()
    for _, store in moves:
        store.wait()


def write_terms(place, pieces, total, low, high, sems, chunk):
    rows, piece, wide = low.shape
    steps = []
    for slot in range(rows):
        owner = place[0] ^ slot if chunk else (place[1] - slot) & (rows - 1)
        start = pl.multiple_of(owner * piece, 16)
        fetch = pltpu.make_async_copy(pieces[slot], low.at[slot], sems.at[0, slot])
        store = pltpu.make_async_copy(
            high.at[slot],
            total.at[pl.ds(start, piece), chunk * wide : (chunk + 1) * wide],
            sems.at[1, slot],
        )
        steps.append((fetch, store))
    for fetch, _ in steps:
        fetch.start()

    def rest():
        for slot, (fetch, store) in enumerate(steps):
            fetch.wait()
            high[slot] = low[slot].astype(jnp.float32)
            store.start()
        return [store for _, store in steps]

    return rest


def finish(place, parts, pieces, chunks):
    rows = len(parts)
    _, tokens, width = parts[0].shape
    piece, wide = pieces[0].shape

    def body(place_ref, *refs):
        ins, terms, outs, total = refs[:rows], refs[rows : 2 * rows], refs[2 * rows :][:3], refs[-6]
        held, low, high, sems, term_sems = refs[-5:]
        moves = []
        for slot in range(rows):
            start = pl.multiple_of((place_ref[0] ^ slot) * width, HDIM)
            for at in range(3):
                box = held.at[slot, at]
                moves.append(
                    (
                        pltpu.make_async_copy(ins[slot].at[at], box, sems.at[0, slot, at]),
                        pltpu.make_async_copy(
                            box, outs[at].at[0, :, pl.ds(start, width)], sems.at[1, slot, at]
                        ),
                    )
                )
        rest = write_terms(place_ref, terms, total, low, high, term_sems, 0)
        run(moves, rest)

    full = jax.ShapeDtypeStruct((1, tokens, width * rows), parts[0].dtype)
    return pl.pallas_call(
        body,
        grid_spec=pltpu.PrefetchScalarGridSpec(
            num_scalar_prefetch=1,
            grid=(1,),
            in_specs=[pl.BlockSpec(memory_space=pltpu.HBM)] * (2 * rows),
            out_specs=[pl.BlockSpec(memory_space=pltpu.HBM)] * 4,
            scratch_shapes=[
                pltpu.VMEM((rows, 3, tokens, width), parts[0].dtype),
                pltpu.VMEM((rows, piece, wide), pieces[0].dtype),
                pltpu.VMEM((rows, piece, wide), jnp.float32),
                pltpu.SemaphoreType.DMA((2, rows, 3)),
                pltpu.SemaphoreType.DMA((2, rows)),
            ],
        ),
        out_shape=[full] * 3 + [jax.ShapeDtypeStruct((rows * piece, chunks * wide), jnp.float32)],
        cost_estimate=cost(0, 12 * tokens * width * rows + 6 * rows * piece * wide),
        name="finish",
    )(place, *parts, *pieces)


def finish_terms(place, total, pieces, chunk):
    rows = len(pieces)
    piece, wide = pieces[0].shape

    def body(place_ref, _, *refs):
        terms, (out, low, high, sems) = refs[:rows], refs[rows:]
        for store in write_terms(place_ref, terms, out, low, high, sems, chunk)():
            store.wait()

    return pl.pallas_call(
        body,
        grid_spec=pltpu.PrefetchScalarGridSpec(
            num_scalar_prefetch=1,
            grid=(1,),
            in_specs=[pl.BlockSpec(memory_space=pltpu.HBM)] * (1 + rows),
            out_specs=pl.BlockSpec(memory_space=pltpu.HBM),
            scratch_shapes=[
                pltpu.VMEM((rows, piece, wide), pieces[0].dtype),
                pltpu.VMEM((rows, piece, wide), jnp.float32),
                pltpu.SemaphoreType.DMA((2, rows)),
            ],
        ),
        out_shape=jax.ShapeDtypeStruct(total.shape, total.dtype),
        input_output_aliases={1: 0},
        cost_estimate=cost(0, 6 * rows * piece * wide),
        name="finish_terms",
    )(place, total, *pieces)


def forward(parts):
    rows = len(parts)
    _, tokens, width = parts[0].shape
    length, heads = rows * tokens, width // HDIM
    scale = math.log2(math.e) / math.sqrt(HDIM)

    def body(*refs):
        ins, (probs_ref, attended_ref) = refs[:rows], refs[rows:]
        keys = jnp.concatenate([ref[1] for ref in ins], axis=0)
        values = jnp.concatenate([ref[2] for ref in ins], axis=0).T
        for slot in range(rows):
            across = slice(slot * tokens, (slot + 1) * tokens)
            scores = dot(keys, ins[slot][0], NT)
            top = jnp.max(scores, axis=0, keepdims=True)
            powers = jnp.exp2((scores - top) * scale)
            total = jnp.sum(powers, axis=0, keepdims=True)
            probs = (powers * (1.0 / total)).astype(jnp.bfloat16)
            probs_ref[0, :, across] = probs
            attended_ref[:, across] = dot(values, probs).astype(jnp.bfloat16)

    part = pl.BlockSpec((3, tokens, HDIM), lambda h: (0, 0, h))
    return pl.pallas_call(
        body,
        grid=(heads,),
        in_specs=[part] * rows,
        out_specs=[
            pl.BlockSpec((1, length, length), lambda h: (h, 0, 0)),
            pl.BlockSpec((HDIM, length), lambda h: (h, 0)),
        ],
        out_shape=[
            jax.ShapeDtypeStruct((heads, length, length), jnp.bfloat16),
            jax.ShapeDtypeStruct((width, length), jnp.bfloat16),
        ],
        cost_estimate=cost(
            8 * heads * length * length * HDIM, 2 * heads * length * length, heads * length * length
        ),
        name="forward",
    )(*parts)


def backward(parts, probs, grad_attn, first, count):
    rows = len(parts)
    tokens = parts[0].shape[1]
    length = rows * tokens
    factor = 1.0 / math.sqrt(HDIM)

    def body(*refs):
        ins, (probs_ref, grad_ref) = refs[:rows], refs[rows : rows + 2]
        outs, scores_ref = refs[rows + 2 : -1], refs[-1]
        queries = jnp.concatenate([ref[0] for ref in ins], axis=0)
        keys = jnp.concatenate([ref[1] for ref in ins], axis=0).T
        values = jnp.concatenate([ref[2] for ref in ins], axis=0)
        for slot in range(rows):
            across = slice(slot * tokens, (slot + 1) * tokens)
            probs = probs_ref[0, :, across].astype(jnp.float32)
            terms = probs * dot(values, grad_ref[:, across])
            centre = jnp.sum(terms, axis=0, keepdims=True)
            scores_ref[:, across] = (terms - probs * centre).astype(jnp.bfloat16)
        scores = scores_ref[...]
        grad_query = (dot(keys, scores) * factor).T
        grad_key = dot(scores, queries) * factor
        grad_value = dot(probs_ref[0], grad_ref[...], NT)
        for slot in range(rows):
            down = slice(slot * tokens, (slot + 1) * tokens)
            outs[slot][0] = grad_query[down].astype(jnp.bfloat16)
            outs[slot][1] = grad_key[down].astype(jnp.bfloat16)
            outs[slot][2] = grad_value[down].astype(jnp.bfloat16)

    part = pl.BlockSpec((3, tokens, HDIM), lambda i: (0, 0, first + i))
    shape = (3, tokens, count * HDIM)
    return pl.pallas_call(
        body,
        grid=(count,),
        in_specs=[part] * rows
        + [
            pl.BlockSpec((1, length, length), lambda i: (first + i, 0, 0)),
            pl.BlockSpec((HDIM, length), lambda i: (first + i, 0)),
        ],
        out_specs=[pl.BlockSpec((3, tokens, HDIM), lambda i: (0, 0, i))] * rows,
        out_shape=[jax.ShapeDtypeStruct(shape, jnp.bfloat16)] * rows,
        scratch_shapes=[pltpu.VMEM((length, length), jnp.bfloat16)],
        cost_estimate=cost(8 * count * length * length * HDIM, 2 * count * length * length),
        name="backward",
    )(*parts, probs, grad_attn)


def stacked(refs):
    return jnp.concatenate([ref[...] for ref in refs], axis=0)


def project(place, weights, grads):
    chunks, count = len(grads), len(grads[0])
    half, depth = weights[0].shape
    half = half * len(weights) // 2
    step = grads[0][0].shape[1] // 2

    def body(place_ref, *refs):
        ins, out, total = refs[len(weights) : -2], refs[-2], refs[-1]
        at = pl.program_id(0)
        lines = stacked(refs[: len(weights)])
        for chunk in range(chunks):

            @pl.when(at // 2 == chunk)
            def _():
                term = dot(lines, stacked(ins[chunk * count : (chunk + 1) * count]), NT)
                if chunk:
                    total[...] += term
                else:
                    total[...] = jnp.where(at == 0, 0.0, total[...]) + term

        @pl.when(at == chunks * 2 - 1)
        def _():
            for core in range(2):

                @pl.when(place_ref[2] == core)
                def _():
                    out[core * half : (core + 1) * half] = total[:half].astype(out.dtype)
                    out[(1 - core) * half : (2 - core) * half] = total[half:].astype(out.dtype)

    def block_of(chunk, block):
        return pl.BlockSpec(
            (block.shape[0], step), lambda i, place_ref: (0, jnp.clip(i - chunk * 2, 0, 1))
        )

    shape = (2 * half, sum(block.shape[0] for block in grads[0]))
    return pl.pallas_call(
        body,
        grid_spec=pltpu.PrefetchScalarGridSpec(
            num_scalar_prefetch=1,
            grid=(chunks * 2,),
            in_specs=[
                pl.BlockSpec((part.shape[0], step), lambda i, place_ref: (0, i)) for part in weights
            ]
            + [block_of(chunk, block) for chunk in range(chunks) for block in grads[chunk]],
            out_specs=whole(shape),
            scratch_shapes=[pltpu.VMEM(shape, jnp.float32)],
        ),
        out_shape=jax.ShapeDtypeStruct(shape, jnp.bfloat16),
        cost_estimate=cost(2 * shape[0] * shape[1] * depth, 2 * depth * (shape[0] + shape[1])),
        name="project",
    )(place, *weights, *(block for chunk in grads for block in chunk))


def weight_terms(place, attended, grads, parts, by_plane):
    width, length = attended.shape
    step = grads[0].shape[1] // 2
    piece = width // 2 // parts

    def body(place_ref, attended_ref, *refs):
        ins, (keep, give) = refs[:-2], refs[-2:]
        term = dot(attended_ref[...], stacked(ins)).astype(jnp.bfloat16)
        row, plane, core = place_ref[0], place_ref[1], place_ref[2]
        for side in range(2):
            for out, mine in ((keep, core == side), (give, core != side)):

                @pl.when(mine)
                def _():
                    for at in range(parts):
                        start = (side * parts + at) * piece
                        slot = (at - plane) & (parts - 1) if by_plane else at ^ row
                        out[slot] = term[start : start + piece]

    shape = jax.ShapeDtypeStruct((parts, piece, 2 * step), jnp.bfloat16)
    spec = pl.BlockSpec((parts, piece, step), lambda i, place_ref: (0, 0, i))
    return pl.pallas_call(
        body,
        grid_spec=pltpu.PrefetchScalarGridSpec(
            num_scalar_prefetch=1,
            grid=(2,),
            in_specs=[whole((width, length))]
            + [pl.BlockSpec((block.shape[0], step), lambda i, place_ref: (0, i)) for block in grads],
            out_specs=[spec] * 2,
        ),
        out_shape=[shape] * 2,
        cost_estimate=cost(4 * width * length * step, 2 * (width * length + 2 * length * step)),
        name="weight_terms",
    )(place, attended, *grads)


def after(value, *done):
    return lax.optimization_barrier((value, done))[0]


def onward(planes, hop, z, c, r):
    to = z + 1 if z > r else z - 1
    return (to, c, r) if abs(z - r) == hop and 0 <= to < planes else None


def by_heads(fsdp, rows, query_rows, key_rows, value_rows, grad_out, w_out):
    planes = fsdp // 2
    row = lax.axis_index("rows")
    member = lax.axis_index("fsdp")
    plane, core = member // 2, member % 2
    place = jnp.stack([row, plane, core]).astype(jnp.int32)

    def send(array, target):
        pairs = []
        for z in range(planes):
            for c in range(2):
                for r in range(rows):
                    to = target(z, c, r)
                    if to is not None:
                        pairs.append(((z * 2 + c) * rows + r, (to[0] * 2 + to[1]) * rows + to[2]))
        return lax.ppermute(array, ("fsdp", "rows"), pairs)

    def to_row(array, slot):
        return send(array, lambda z, c, r: (z, c, r ^ slot))

    def to_core(array):
        return send(array, lambda z, c, r: (z, 1 - c, r))

    def to_plane(array, ahead):
        return send(array, lambda z, c, r: ((z + ahead) % planes, c, r))

    grad_flat = grad_out[0]
    wide = grad_flat.shape[1] // 2

    def gather(chunk, *done):
        by_x, by_y = to_row(chunk, 1), to_row(chunk, 2)
        by_x, by_y = after((by_x, by_y), *done)
        cut = chunk.shape[0] // 2
        upper, lower = by_x[:cut], by_y[cut:]
        by_both = [to_row(upper, 2), to_row(lower, 1)]
        return [chunk, by_x, by_y, *by_both]

    grads = [gather(grad_flat[:, :wide])]

    away = jnp.abs(plane - row)
    cut = w_out.shape[0] // 2

    def leave(lines):
        above = send(lines, lambda z, c, r: (z + 1, c, r) if z == r and z + 1 < planes else None)
        below = send(lines, lambda z, c, r: (z - 1, c, r) if z == r and z > 0 else None)
        return jnp.where(plane > row, above, below)

    def go_on(hop, lines):
        return send(lines, functools.partial(onward, planes, hop))

    first = [w_out[:cut]]
    first.append(leave(first[0]))
    first.append(go_on(1, first[1]))
    second = [w_out[cut:]]
    second.append(leave(after(second[0], first[1])))
    first.append(go_on(2, first[2]))
    second.append(go_on(1, second[1]))

    packed = pack(place, query_rows, key_rows, value_rows, rows)
    parts = [packed[0]] + [to_row(packed[slot], slot) for slot in range(1, rows)]
    probs, attended = forward(parts)
    second.append(go_on(2, after(second[2], attended)))

    def mine(stages):
        here = stages[0]
        for hop in range(1, planes):
            here = jnp.where(away == hop, stages[hop], here)
        return here

    grads.append(gather(after(grad_flat[:, wide:], parts), attended))


    def reduce_cores(at, attended, chunk):
        keep, give = weight_terms(place, attended, chunk, rows, not at)
        return keep, to_core(give)

    def add_cores(keep, got):
        return [
            (keep[slot].astype(jnp.float32) + got[slot].astype(jnp.float32)).astype(jnp.bfloat16)
            for slot in range(rows)
        ]

    def to_rows(blocks):
        return [blocks[0]] + [to_row(blocks[slot], slot) for slot in range(1, rows)]

    def to_planes(blocks):
        return [blocks[0]] + [to_plane(blocks[ahead], ahead) for ahead in range(1, planes)]

    def by_plane(blocks):
        return [
            lax.select_n(((plane + ahead) % planes) ^ row, *blocks) for ahead in range(planes)
        ]

    def added(blocks):
        total = blocks[0].astype(jnp.float32)
        for block in blocks[1:]:
            total = total + block.astype(jnp.float32)
        return total.astype(jnp.bfloat16)

    early = to_planes(add_cores(*reduce_cores(0, attended, grads[0])))
    first[-1], second[-1] = after((first[-1], second[-1]), early[0])
    weights = [mine(first), mine(second)]
    weights += [to_core(part) for part in weights]
    late = reduce_cores(1, after(attended, weights), grads[1])
    grad_attn = project(place, weights, grads)
    late = to_rows(add_cores(*after(late, grad_attn)))
    early = to_rows([added(after(early, grad_attn))] * rows)
    sent = backward(parts, probs, grad_attn, 0, probs.shape[0])
    back = to_rows(sent)
    late = to_planes(by_plane(after(late, sent[0])))
    early = to_planes(by_plane(after(early, sent[0])))
    late = to_rows([added(late)] * rows)
    *outs, total = finish(place, back, early, len(grads))
    return (*outs, finish_terms(place, total, after(late, outs[0]), 1))


def by_tokens(query_rows, key_rows, value_rows, grad_out, w_out):
    tokens, width = query_rows.shape[1:]
    heads = width // HDIM
    factor = 1.0 / math.sqrt(HDIM)
    grad_flat = grad_out[0]
    groups = math.gcd(heads, 3)

    def split(array, count):
        return jnp.moveaxis(array.reshape(count, groups, heads // groups, HDIM), 1, 0)

    def join(array, count):
        return jnp.moveaxis(array, 0, 1).reshape(count, width)

    grad_attn = lax.dot_general(
        grad_flat,
        lax.all_gather(w_out, "fsdp", axis=0, tiled=True),
        NT,
        preferred_element_type=jnp.float32,
    ).astype(jnp.bfloat16)
    all_keys = lax.all_gather(key_rows, "rows", axis=1, tiled=True)
    all_values = lax.all_gather(value_rows, "rows", axis=1, tiled=True)
    length = all_keys.shape[1]

    def product(spec, a, b):
        return jnp.einsum(spec, a, b, preferred_element_type=jnp.float32)

    def attend(inputs):
        queries, keys, values, grads = inputs
        probs = jax.nn.softmax(product("qhd,khd->hqk", queries, keys) * factor, axis=-1)
        low = probs.astype(jnp.bfloat16)
        attended = product("hqk,khd->qhd", low, values)
        value_part = product("hqk,qhd->khd", low, grads)
        grad_probs = product("qhd,khd->hqk", grads, values)
        centre = jnp.sum(probs * grad_probs, axis=-1, keepdims=True)
        grad_scores = (probs * (grad_probs - centre)).astype(jnp.bfloat16)
        grad_query = product("hqk,khd->qhd", grad_scores, keys) * factor
        key_part = product("hqk,qhd->khd", grad_scores, queries) * factor
        return (
            attended.astype(jnp.bfloat16),
            grad_query.astype(jnp.bfloat16),
            key_part.astype(jnp.bfloat16),
            value_part.astype(jnp.bfloat16),
        )

    attended, grad_query, key_part, value_part = lax.map(
        attend,
        (
            split(query_rows[0], tokens),
            split(all_keys[0], length),
            split(all_values[0], length),
            split(grad_attn, tokens),
        ),
    )

    def scatter(part):
        part = join(part, length).reshape(1, length, width)
        return lax.psum_scatter(part, "rows", scatter_dimension=1, tiled=True)

    term = lax.dot_general(
        join(attended, tokens),
        grad_flat,
        (((0,), (0,)), ((), ())),
        preferred_element_type=jnp.float32,
    ).astype(jnp.bfloat16)
    share = lax.psum_scatter(term, "fsdp", scatter_dimension=0, tiled=True)
    grad_w_out = lax.psum(share, "rows").astype(jnp.float32)
    return (
        join(grad_query, tokens).reshape(1, tokens, width),
        scatter(key_part),
        scatter(value_part),
        grad_w_out,
    )


def solution(mesh):
    fsdp, rows = mesh.shape["fsdp"], mesh.shape["rows"]

    def local(query_rows, key_rows, value_rows, grad_out, w_out):
        heads = query_rows.shape[2] // HDIM
        if rows == 4 and fsdp == 2 * rows and heads % rows == 0:
            plan = functools.partial(by_heads, fsdp, rows)
        else:
            plan = by_tokens
        return plan(query_rows, key_rows, value_rows, grad_out, w_out)

    tokens = P("fsdp", "rows", None)
    return jax.shard_map(
        local,
        mesh=mesh,
        in_specs=(tokens, tokens, tokens, tokens, P("fsdp", None)),
        out_specs=(tokens, tokens, tokens, P("fsdp", None)),
        check_vma=False,
    )
```

profile of v0, /device:TPU:0, one launch (start us, length us, event | category | flops | bytes accessed | tf_op | source)
XLA Modules:
  0.0 220.7 jit_solution(10768255584660711145)
XLA Ops:
  0.6 2.5 %fusion.9 = (bf16[96,3072]{1,0:T(8,128)(2,1)}, bf16[96,3072]{1,0:T(8,128)(2,1)}) fusion(bf16[192,3072]{1,0:T(8,128)(2,1)} %param.9), kind=kLoop, calls=%fused_computation.31 | loop fusion | bytes 2359296 | tf_op jit(solution)/shard_map/slice | solution.py:424
  3.2 5.8 %collective-permute-start.3 = (bf16[96,3072]{1,0:T(8,128)(2,1)}, bf16[96,3072]{1,0:T(8,128)(2,1)}, u32[]{:S(2)}, u32[]{:S(2)}) collective-permute-start(bf16[96,3072]{1,0:T(8,128)(2,1)} %get-tuple-element.109), channel_id=1, source_target_pairs={{0,8},{4,12},{9,17},{13,21},{18,26},{22,30}} | collective-permute-start | bytes 1769480 | tf_op jit(solution)/shard_map/ppermute | solution.py:386
  8.9 1.5 collective-permute-start.4
  10.8 0.7 pad_add_fusion.place_ref
  11.6 3.3 %pack.1 = (bf16[3,256,384]{2,1,0:T(8,128)(2,1)}, bf16[3,256,384]{2,1,0:T(8,128)(2,1)}, bf16[3,256,384]{2,1,0:T(8,128)(2,1)}, bf16[3,256,384]{2,1,0:T(8,128)(2,1)}) custom-call(s32[3]{0:T(128)} %pad_add_fusion.place_ref, bf16[1,256,1536]{2,1,0:T(8,128)(2,1)} %refs_0_.1, bf16[1,256,1536]{2,1,0:T(8,128)(2,1)} %refs_1_.1, bf16[1,256,1536]{2,1,0:T(8,128)(2,1)} %refs_2_.1), custom_call_target="tpu_custom_call" | custom-call | bytes 4718592 | tf_op jit(solution)/shard_map/pack/pallas_call | solution.py:52
  14.9 1.7 collective-permute-start
  16.6 4.4 %collective-permute-done.3 = bf16[96,3072]{1,0:T(8,128)(2,1)} collective-permute-done((bf16[96,3072]{1,0:T(8,128)(2,1)}, bf16[96,3072]{1,0:T(8,128)(2,1)}, u32[]{:S(2)}, u32[]{:S(2)}) %collective-permute-start.3) | collective-permute-done | bytes 589856 | tf_op jit(solution)/shard_map/ppermute | solution.py:386
  21.0 2.0 broadcast_select_fusion.1
  23.0 20.8 %collective-permute-done.refs_1_ = bf16[3,256,384]{2,1,0:T(8,128)(2,1)} collective-permute-done((bf16[3,256,384]{2,1,0:T(8,128)(2,1)}, bf16[3,256,384]{2,1,0:T(8,128)(2,1)}, u32[]{:S(2)}, u32[]{:S(2)}) %collective-permute-start) | collective-permute-done | bytes 589856 | tf_op jit(solution)/shard_map/ppermute | solution.py:386
  43.8 4.4 %collective-permute-start.7 = (bf16[96,3072]{1,0:T(8,128)(2,1)}, bf16[96,3072]{1,0:T(8,128)(2,1)}, u32[]{:S(2)}, u32[]{:S(2)}) collective-permute-start(bf16[96,3072]{1,0:T(8,128)(2,1)} %get-tuple-element.55), channel_id=1, source_target_pairs={{0,8},{4,12},{9,17},{13,21},{18,26},{22,30}} | collective-permute-start | bytes 1769480 | tf_op jit(solution)/shard_map/ppermute | solution.py:386
  48.2 6.9 %collective-permute-done.1.refs_2_ = bf16[3,256,384]{2,1,0:T(8,128)(2,1)} collective-permute-done((bf16[3,256,384]{2,1,0:T(8,128)(2,1)}, bf16[3,256,384]{2,1,0:T(8,128)(2,1)}, u32[]{:S(2)}, u32[]{:S(2)}) %collective-permute-start.1) | collective-permute-done | bytes 589856 | tf_op jit(solution)/shard_map/ppermute | solution.py:386
  55.1 1.5 collective-permute-start.8
  56.6 1.5 collective-permute-start.5
  58.1 12.6 %forward.1 = (bf16[3,1024,1024]{2,1,0:T(8,128)(2,1)}, bf16[384,1024]{1,0:T(8,128)(2,1)}) custom-call(bf16[3,256,384]{2,1,0:T(8,128)(2,1)} %get-tuple-element.50.refs_0_, bf16[3,256,384]{2,1,0:T(8,128)(2,1)} %collective-permute-done.refs_1_, bf16[3,256,384]{2,1,0:T(8,128)(2,1)} %collective-permute-done.1.refs_2_, ...), custom_call_target="tpu_custom_call" | custom-call | flops 3221225472 | bytes 6291456 | tf_op jit(solution)/shard_map/forward/pallas_call | solution.py:204
  70.8 2.0 collective-permute-start.14
  72.9 1.1 broadcast_select_fusion
  74.0 1.5 collective-permute-start.9
  75.5 5.0 %collective-permute-done.13.refs_3_.refs_7_ = bf16[128,1536]{1,0:T(8,128)(2,1)S(1)} collective-permute-done((bf16[128,1536]{1,0:T(8,128)(2,1)S(1)}, bf16[128,1536]{1,0:T(8,128)(2,1)S(1)}, u32[]{:S(2)}, u32[]{:S(2)}) %collective-permute-start.13) | collective-permute-done | bytes 393248 | tf_op jit(solution)/shard_map/ppermute | solution.py:386
  80.7 0.5 copy-done.19
  81.3 5.2 %weight_terms.2 = (bf16[4,48,1536]{2,1,0:T(8,128)(2,1)}, bf16[4,48,1536]{2,1,0:T(8,128)(2,1)}) custom-call(s32[3]{0:T(128)} %pad_add_fusion.place_ref, bf16[384,1024]{1,0:T(8,128)(2,1)} %get-tuple-element.83.attended_ref, bf16[256,1536]{1,0:T(8,128)(2,1)} %copy-done.2, bf16[256,1536]{1,0:T(8,128)(2,1)} %copy-done.7, bf16[256,1536]{1,0:T(8,128)(2,1)} %copy-done.8, ...), custom_call_target="tpu_custom_call" | custom-call | flops 1207959552 | bytes 3932160 | tf_op jit(solution)/shard_map/weight_terms/pallas_call | solution.py:347
  86.6 1.6 collective-permute-start.6
  88.2 1.5 collective-permute-start.10
  89.7 1.2 collective-permute-start.18
  90.9 2.1 collective-permute-start.19
  93.1 2.0 fusion.3
  95.5 0.5 collective-permute-start.17
  96.0 13.5 %collective-permute-done.18.refs_10_.refs_1_ = bf16[256,1536]{1,0:T(8,128)(2,1)S(1)} collective-permute-done((bf16[256,1536]{1,0:T(8,128)(2,1)S(1)}, bf16[256,1536]{1,0:T(8,128)(2,1)S(1)}, u32[]{:S(2)}, u32[]{:S(2)}) %collective-permute-start.18) | collective-permute-done | bytes 786464 | tf_op jit(solution)/shard_map/ppermute | solution.py:386
  109.5 0.9 collective-permute-done.19.refs_11_.refs_2_
  110.5 0.8 slice.80
  111.3 1.2 collective-permute-start.20
  112.5 0.8 slice.81
  113.3 11.8 %collective-permute-start.21 = (bf16[128,1536]{1,0:T(8,128)(2,1)}, bf16[128,1536]{1,0:T(8,128)(2,1)S(1)}, u32[]{:S(2)}, u32[]{:S(2)}) collective-permute-start(bf16[128,1536]{1,0:T(8,128)(2,1)} %slice.81), channel_id=1, source_target_pairs={{0,1},{1,0},{2,3},{3,2},{4,5},{5,4},{6,7},{7,6},{8,9},{9,8},{10,11... | collective-permute-start | bytes 1179656 | tf_op jit(solution)/shard_map/ppermute | solution.py:386
  125.0 11.3 %collective-permute-start.26 = (bf16[48,1536]{1,0:T(8,128)(2,1)}, bf16[48,1536]{1,0:T(8,128)(2,1)}, u32[]{:S(2)}, u32[]{:S(2)}) collective-permute-start(bf16[48,1536]{1,0:T(8,128)(2,1)} %get-tuple-element.103), channel_id=1, source_target_pairs={{0,16},{1,17},{2,18},{3,19},{4,20},{5,21},{6,22},{7,23},{8,24},{9,... | collective-permute-start | bytes 442376 | tf_op jit(solution)/shard_map/ppermute | solution.py:386
  136.4 2.9 %collective-permute-start.27 = (bf16[48,1536]{1,0:T(8,128)(2,1)S(1)}, bf16[48,1536]{1,0:T(8,128)(2,1)}, u32[]{:S(2)}, u32[]{:S(2)}) collective-permute-start(bf16[48,1536]{1,0:T(8,128)(2,1)S(1)} %get-tuple-element.102), channel_id=1, source_target_pairs={{0,24},{1,25},{2,26},{3,27},{4,28},{5,29},{6,30},{7,31},{8,0},{9,1... | collective-permute-start | bytes 442376 | tf_op jit(solution)/shard_map/ppermute | solution.py:386
  139.3 0.8 copy-done.12
  140.1 0.8 copy-done.13
  140.9 8.0 %project.1.refs_5_ = bf16[384,1024]{1,0:T(8,128)(2,1)} custom-call(s32[3]{0:T(128)} %pad_add_fusion.place_ref, bf16[96,3072]{1,0:T(8,128)(2,1)} %copy-done.4, bf16[96,3072]{1,0:T(8,128)(2,1)} %copy-done.3, bf16[96,3072]{1,0:T(8,128)(2,1)} %copy-done.12, bf16[96,3072]{1,0:T(8,128)(2,1)} %copy-done.13, bf16[256,1536]{1,0:T(8,128)(2,1)} %copy-done.2, ...), custom_call_target="tpu_custom_call" | custom-call | flops 2415919104 | bytes 8650752 | tf_op jit(solution)/shard_map/project/pallas_call | solution.py:308
  149.0 5.2 %weight_terms.3 = (bf16[4,48,1536]{2,1,0:T(8,128)(2,1)}, bf16[4,48,1536]{2,1,0:T(8,128)(2,1)}) custom-call(s32[3]{0:T(128)} %pad_add_fusion.place_ref, bf16[384,1024]{1,0:T(8,128)(2,1)} %get-tuple-element.83.attended_ref, bf16[256,1536]{1,0:T(8,128)(2,1)} %copy-done.1, bf16[256,1536]{1,0:T(8,128)(2,1)} %copy-done.9, bf16[256,1536]{1,0:T(8,128)(2,1)} %copy-done.10, ...), custom_call_target="tpu_custom_call" | custom-call | flops 1207959552 | bytes 3932160 | tf_op jit(solution)/shard_map/weight_terms/pallas_call | solution.py:347
  154.2 1.1 add_convert_fusion.5
  155.3 0.3 collective-permute-start.28
  155.7 1.6 collective-permute-start.29
  157.3 1.6 collective-permute-start.30
  158.9 11.4 %backward.1 = (bf16[3,256,384]{2,1,0:T(8,128)(2,1)}, bf16[3,256,384]{2,1,0:T(8,128)(2,1)}, bf16[3,256,384]{2,1,0:T(8,128)(2,1)}, bf16[3,256,384]{2,1,0:T(8,128)(2,1)}) custom-call(bf16[3,256,384]{2,1,0:T(8,128)(2,1)} %get-tuple-element.50.refs_0_, bf16[3,256,384]{2,1,0:T(8,128)(2,1)} %collective-permute-done.refs_1_, ...), custom_call_target="tpu_custom_call" | custom-call | flops 3221225472 | bytes 6291456 | tf_op jit(solution)/shard_map/backward/pallas_call | solution.py:253
  170.9 1.6 collective-permute-start.36
  172.5 1.6 collective-permute-start.37
  174.1 0.7 select_select_fusion.5
  174.8 2.5 %collective-permute-done.35 = bf16[48,1536]{1,0:T(8,128)(2,1)S(1)} collective-permute-done((bf16[48,1536]{1,0:T(8,128)(2,1)S(1)}, bf16[48,1536]{1,0:T(8,128)(2,1)S(1)}, u32[]{:S(2)}, u32[]{:S(2)}) %collective-permute-start.35) | collective-permute-done | bytes 147488 | tf_op jit(solution)/shard_map/ppermute | solution.py:386
  177.3 2.9 %collective-permute-done.37 = bf16[48,1536]{1,0:T(8,128)(2,1)S(1)} collective-permute-done((bf16[48,1536]{1,0:T(8,128)(2,1)S(1)}, bf16[48,1536]{1,0:T(8,128)(2,1)S(1)}, u32[]{:S(2)}, u32[]{:S(2)}) %collective-permute-start.37) | collective-permute-done | bytes 147488 | tf_op jit(solution)/shard_map/ppermute | solution.py:386
  180.6 1.9 collective-permute-start.38
  182.5 1.7 collective-permute-start.22
  184.2 0.6 collective-permute-start.23
  184.7 1.3 collective-permute-done.40
  186.0 1.7 collective-permute-start.24
  187.7 6.3 %collective-permute-done.39 = bf16[48,1536]{1,0:T(8,128)(2,1)S(1)} collective-permute-done((bf16[48,1536]{1,0:T(8,128)(2,1)S(1)}, bf16[48,1536]{1,0:T(8,128)(2,1)S(1)}, u32[]{:S(2)}, u32[]{:S(2)}) %collective-permute-start.39) | collective-permute-done | bytes 147488 | tf_op jit(solution)/shard_map/ppermute | solution.py:386
  194.0 2.0 collective-permute-start.33
  196.1 6.5 %collective-permute-done.32.refs_6_ = bf16[48,1536]{1,0:T(8,128)(2,1)S(1)} collective-permute-done((bf16[48,1536]{1,0:T(8,128)(2,1)S(1)}, bf16[48,1536]{1,0:T(8,128)(2,1)S(1)}, u32[]{:S(2)}, u32[]{:S(2)}) %collective-permute-start.32) | collective-permute-done | bytes 147488 | tf_op jit(solution)/shard_map/ppermute | solution.py:386
  202.8 2.2 %collective-permute-start.42 = (bf16[48,1536]{1,0:T(8,128)(2,1)S(1)}, bf16[48,1536]{1,0:T(8,128)(2,1)S(1)}, u32[]{:S(2)}, u32[]{:S(2)}) collective-permute-start(bf16[48,1536]{1,0:T(8,128)(2,1)S(1)} %add_convert_fusion.refs_0_), channel_id=1, source_target_pairs={{0,2},{1,3},{2,0},{3,1},{4,6},{5,7},{6,4},{7,5},{8,10},{9,11},{10,... | collective-permute-start | bytes 442376 | tf_op jit(solution)/shard_map/ppermute | solution.py:386
  205.0 1.5 collective-permute-start.43
  206.5 2.2 %collective-permute-done.23.refs_2_ = bf16[3,256,384]{2,1,0:T(8,128)(2,1)S(1)} collective-permute-done((bf16[3,256,384]{2,1,0:T(8,128)(2,1)S(1)}, bf16[3,256,384]{2,1,0:T(8,128)(2,1)S(1)}, u32[]{:S(2)}, u32[]{:S(2)}) %collective-permute-start.23) | collective-permute-done | bytes 589856 | tf_op jit(solution)/shard_map/ppermute | solution.py:386
  208.7 3.5 %collective-permute-done.24.refs_3_ = bf16[3,256,384]{2,1,0:T(8,128)(2,1)S(1)} collective-permute-done((bf16[3,256,384]{2,1,0:T(8,128)(2,1)S(1)}, bf16[3,256,384]{2,1,0:T(8,128)(2,1)S(1)}, u32[]{:S(2)}, u32[]{:S(2)}) %collective-permute-start.24) | collective-permute-done | bytes 589856 | tf_op jit(solution)/shard_map/ppermute | solution.py:386
  212.2 0.8 copy-done.18
  213.0 4.0 %finish.1 = (bf16[1,256,1536]{2,1,0:T(8,128)(2,1)}, bf16[1,256,1536]{2,1,0:T(8,128)(2,1)}, bf16[1,256,1536]{2,1,0:T(8,128)(2,1)}, f32[192,3072]{1,0:T(8,128)}) custom-call(s32[3]{0:T(128)} %pad_add_fusion.place_ref, bf16[3,256,384]{2,1,0:T(8,128)(2,1)} %get-tuple-element.67.refs_0_, bf16[3,256,384]{2,1,0:T(8,128)(2,1)} %copy-done.16, ...), custom_call_target="tpu_custom_call" | custom-call | bytes 6488064 | tf_op jit(solution)/shard_map/finish/pallas_call | solution.py:133
  217.1 0.6 copy-done.25
  217.9 2.7 %finish_terms.1 = f32[192,3072]{1,0:T(8,128)} custom-call(s32[3]{0:T(128)} %pad_add_fusion.place_ref, f32[192,3072]{1,0:T(8,128)} %get-tuple-element.82._, bf16[48,1536]{1,0:T(8,128)(2,1)} %copy-done.14, bf16[48,1536]{1,0:T(8,128)(2,1)} %copy-done.25, bf16[48,1536]{1,0:T(8,128)(2,1)} %copy-done.26, ...), custom_call_target="tpu_custom_call", output_to_operand_aliasing={{}: (1, {})} | custom-call | bytes 1769472 | tf_op jit(solution)/shard_map/finish_terms/pallas_call | solution.py:163
  (110 shorter events, 2.7 us)
Async XLA Ops:
  0.6 9.8 %copy-start.11 = (bf16[1,256,3072]{2,1,0:T(8,128)(2,1)S(1)}, bf16[1,256,3072]{2,1,0:T(8,128)(2,1)}, u32[]{:S(2)}) copy-start(bf16[1,256,3072]{2,1,0:T(8,128)(2,1)} %param.8) | copy-start | bytes 4718596
  3.2 17.8 %collective-permute-start.3 = (bf16[96,3072]{1,0:T(8,128)(2,1)}, bf16[96,3072]{1,0:T(8,128)(2,1)}, u32[]{:S(2)}, u32[]{:S(2)}) collective-permute-start(bf16[96,3072]{1,0:T(8,128)(2,1)} %get-tuple-element.109), channel_id=1, source_target_pairs={{0,8},{4,12},{9,17},{13,21},{18,26},{22,30}} | collective-permute-start | bytes 1769480 | tf_op jit(solution)/shard_map/ppermute | solution.py:386
  8.9 12.1 %collective-permute-start.4 = (bf16[96,3072]{1,0:T(8,128)(2,1)}, bf16[96,3072]{1,0:T(8,128)(2,1)}, u32[]{:S(2)}, u32[]{:S(2)}) collective-permute-start(bf16[96,3072]{1,0:T(8,128)(2,1)} %get-tuple-element.109), channel_id=1, source_target_pairs={{9,1},{13,5},{18,10},{22,14},{27,19},{31,23}} | collective-permute-start | bytes 1769480 | tf_op jit(solution)/shard_map/ppermute | solution.py:386
  10.6 12.5 %copy-start.2 = (bf16[256,1536]{1,0:T(8,128)(2,1)}, bf16[256,1536]{1,0:T(8,128)(2,1)S(1)}, u32[]{:S(2)}) copy-start(bf16[256,1536]{1,0:T(8,128)(2,1)S(1)} %get-tuple-element.97.refs_0_.refs_4_) | copy-start | bytes 2359300
  10.6 80.3 %copy-start.1 = (bf16[256,1536]{1,0:T(8,128)(2,1)}, bf16[256,1536]{1,0:T(8,128)(2,1)S(1)}, u32[]{:S(2)}) copy-start(bf16[256,1536]{1,0:T(8,128)(2,1)S(1)} %get-tuple-element.64.refs_9_.refs_0_) | copy-start | bytes 2359300
  10.6 60.1 %collective-permute-start.11 = (bf16[256,1536]{1,0:T(8,128)(2,1)S(1)}, bf16[256,1536]{1,0:T(8,128)(2,1)S(1)}, u32[]{:S(2)}, u32[]{:S(2)}) collective-permute-start(bf16[256,1536]{1,0:T(8,128)(2,1)S(1)} %get-tuple-element.97.refs_0_.refs_4_), channel_id=1, source_target_pairs={{0,1},{1,0},{2,3},{3,2},{4,5},{5,4},{6,7},{7,6},{8,9},{9,8},{10,11... | collective-permute-start | bytes 2359304 | tf_op jit(solution)/shard_map/ppermute | solution.py:386
  10.7 60.0 %collective-permute-start.12 = (bf16[256,1536]{1,0:T(8,128)(2,1)S(1)}, bf16[256,1536]{1,0:T(8,128)(2,1)S(1)}, u32[]{:S(2)}, u32[]{:S(2)}) collective-permute-start(bf16[256,1536]{1,0:T(8,128)(2,1)S(1)} %get-tuple-element.97.refs_0_.refs_4_), channel_id=1, source_target_pairs={{0,2},{1,3},{2,0},{3,1},{4,6},{5,7},{6,4},{7,5},{8,10},{9,11},{10,... | collective-permute-start | bytes 2359304 | tf_op jit(solution)/shard_map/ppermute | solution.py:386
  14.9 28.9 %collective-permute-start = (bf16[3,256,384]{2,1,0:T(8,128)(2,1)}, bf16[3,256,384]{2,1,0:T(8,128)(2,1)}, u32[]{:S(2)}, u32[]{:S(2)}) collective-permute-start(bf16[3,256,384]{2,1,0:T(8,128)(2,1)} %get-tuple-element.51), channel_id=1, source_target_pairs={{0,1},{1,0},{2,3},{3,2},{4,5},{5,4},{6,7},{7,6},{8,9},{9,8},{10,11... | collective-permute-start | bytes 1769480 | tf_op jit(solution)/shard_map/ppermute | solution.py:386
  21.0 34.1 %collective-permute-start.1 = (bf16[3,256,384]{2,1,0:T(8,128)(2,1)}, bf16[3,256,384]{2,1,0:T(8,128)(2,1)}, u32[]{:S(2)}, u32[]{:S(2)}) collective-permute-start(bf16[3,256,384]{2,1,0:T(8,128)(2,1)} %get-tuple-element.52), channel_id=1, source_target_pairs={{0,2},{1,3},{2,0},{3,1},{4,6},{5,7},{6,4},{7,5},{8,10},{9,11},{10,... | collective-permute-start | bytes 1769480 | tf_op jit(solution)/shard_map/ppermute | solution.py:386
  21.0 35.6 %collective-permute-start.2 = (bf16[3,256,384]{2,1,0:T(8,128)(2,1)}, bf16[3,256,384]{2,1,0:T(8,128)(2,1)}, u32[]{:S(2)}, u32[]{:S(2)}) collective-permute-start(bf16[3,256,384]{2,1,0:T(8,128)(2,1)} %get-tuple-element.53), channel_id=1, source_target_pairs={{0,3},{1,2},{2,1},{3,0},{4,7},{5,6},{6,5},{7,4},{8,11},{9,10},{10,... | collective-permute-start | bytes 1769480 | tf_op jit(solution)/shard_map/ppermute | solution.py:386
  43.8 29.1 %collective-permute-start.7 = (bf16[96,3072]{1,0:T(8,128)(2,1)}, bf16[96,3072]{1,0:T(8,128)(2,1)}, u32[]{:S(2)}, u32[]{:S(2)}) collective-permute-start(bf16[96,3072]{1,0:T(8,128)(2,1)} %get-tuple-element.55), channel_id=1, source_target_pairs={{0,8},{4,12},{9,17},{13,21},{18,26},{22,30}} | collective-permute-start | bytes 1769480 | tf_op jit(solution)/shard_map/ppermute | solution.py:386
  55.1 17.7 %collective-permute-start.8 = (bf16[96,3072]{1,0:T(8,128)(2,1)}, bf16[96,3072]{1,0:T(8,128)(2,1)}, u32[]{:S(2)}, u32[]{:S(2)}) collective-permute-start(bf16[96,3072]{1,0:T(8,128)(2,1)} %get-tuple-element.55), channel_id=1, source_target_pairs={{9,1},{13,5},{18,10},{22,14},{27,19},{31,23}} | collective-permute-start | bytes 1769480 | tf_op jit(solution)/shard_map/ppermute | solution.py:386
  56.6 29.9 %collective-permute-start.5 = (bf16[96,3072]{1,0:T(8,128)(2,1)}, bf16[96,3072]{1,0:T(8,128)(2,1)}, u32[]{:S(2)}, u32[]{:S(2)}) collective-permute-start(bf16[96,3072]{1,0:T(8,128)(2,1)} %broadcast_select_fusion.1), channel_id=1, source_target_pairs={{8,16},{10,2},{12,20},{14,6},{17,25},{19,11},{21,29},{23,15}} | collective-permute-start | bytes 1769480 | tf_op jit(solution)/shard_map/ppermute | solution.py:386
  70.7 3.3 %copy-start.7 = (bf16[256,1536]{1,0:T(8,128)(2,1)}, bf16[256,1536]{1,0:T(8,128)(2,1)S(1)}, u32[]{:S(2)}) copy-start(bf16[256,1536]{1,0:T(8,128)(2,1)S(1)} %collective-permute-done.11.refs_1_.refs_5_) | copy-start | bytes 2359300
  70.7 9.8 %collective-permute-start.13 = (bf16[128,1536]{1,0:T(8,128)(2,1)S(1)}, bf16[128,1536]{1,0:T(8,128)(2,1)S(1)}, u32[]{:S(2)}, u32[]{:S(2)}) collective-permute-start(bf16[128,1536]{1,0:T(8,128)(2,1)S(1)} %slice.75), channel_id=1, source_target_pairs={{0,2},{1,3},{2,0},{3,1},{4,6},{5,7},{6,4},{7,5},{8,10},{9,11},{10,... | collective-permute-start | bytes 1179656 | tf_op jit(solution)/shard_map/ppermute | solution.py:386
  70.8 9.9 %collective-permute-start.14 = (bf16[128,1536]{1,0:T(8,128)(2,1)S(1)}, bf16[128,1536]{1,0:T(8,128)(2,1)}, u32[]{:S(2)}, u32[]{:S(2)}) collective-permute-start(bf16[128,1536]{1,0:T(8,128)(2,1)S(1)} %slice.76), channel_id=1, source_target_pairs={{0,1},{1,0},{2,3},{3,2},{4,5},{5,4},{6,7},{7,6},{8,9},{9,8},{10,11... | collective-permute-start | bytes 1179656 | tf_op jit(solution)/shard_map/ppermute | solution.py:386
  74.0 12.5 %copy-start.5 = (bf16[96,3072]{1,0:T(8,128)(2,1)}, bf16[96,3072]{1,0:T(8,128)(2,1)S(1)}, u32[]{:S(2)}) copy-start(bf16[96,3072]{1,0:T(8,128)(2,1)S(1)} %broadcast_select_fusion) | copy-start | bytes 1769476
  74.0 14.2 %collective-permute-start.9 = (bf16[96,3072]{1,0:T(8,128)(2,1)S(1)}, bf16[96,3072]{1,0:T(8,128)(2,1)}, u32[]{:S(2)}, u32[]{:S(2)}) collective-permute-start(bf16[96,3072]{1,0:T(8,128)(2,1)S(1)} %broadcast_select_fusion), channel_id=1, source_target_pairs={{8,16},{10,2},{12,20},{14,6},{17,25},{19,11},{21,29},{23,15}} | collective-permute-start | bytes 1769480 | tf_op jit(solution)/shard_map/ppermute | solution.py:386
  86.5 8.6 %copy-start = (bf16[192,3072]{1,0:T(8,128)(2,1)S(1)}, bf16[192,3072]{1,0:T(8,128)(2,1)}, u32[]{:S(2)}) copy-start(bf16[192,3072]{1,0:T(8,128)(2,1)} %param.9) | copy-start | bytes 3538948
  86.5 6.6 %collective-permute-start.15 = (bf16[4,48,1536]{2,1,0:T(8,128)(2,1)}, bf16[4,48,1536]{2,1,0:T(8,128)(2,1)S(1)}, u32[]{:S(2)}, u32[]{:S(2)}) collective-permute-start(bf16[4,48,1536]{2,1,0:T(8,128)(2,1)} %get-tuple-element.61), channel_id=1, source_target_pairs={{0,4},{1,5},{2,6},{3,7},{4,0},{5,1},{6,2},{7,3},{8,12},{9,13},{10,... | collective-permute-start | bytes 1769480 | tf_op jit(solution)/shard_map/ppermute | solution.py:386
  86.6 8.5 %collective-permute-start.6 = (bf16[96,3072]{1,0:T(8,128)(2,1)}, bf16[96,3072]{1,0:T(8,128)(2,1)}, u32[]{:S(2)}, u32[]{:S(2)}) collective-permute-start(bf16[96,3072]{1,0:T(8,128)(2,1)} %collective-permute-done.5), channel_id=1, source_target_pairs={{11,3},{15,7},{16,24},{20,28}} | collective-permute-start | bytes 1769480 | tf_op jit(solution)/shard_map/ppermute | solution.py:386
  88.2 6.8 %collective-permute-start.10 = (bf16[96,3072]{1,0:T(8,128)(2,1)}, bf16[96,3072]{1,0:T(8,128)(2,1)}, u32[]{:S(2)}, u32[]{:S(2)}) collective-permute-start(bf16[96,3072]{1,0:T(8,128)(2,1)} %collective-permute-done.9), channel_id=1, source_target_pairs={{11,3},{15,7},{16,24},{20,28}} | collective-permute-start | bytes 1769480 | tf_op jit(solution)/shard_map/ppermute | solution.py:386
  89.7 5.4 %copy-start.6 = (bf16[96,3072]{1,0:T(8,128)(2,1)S(1)}, bf16[96,3072]{1,0:T(8,128)(2,1)}, u32[]{:S(2)}) copy-start(bf16[96,3072]{1,0:T(8,128)(2,1)} %copy-done.5) | copy-start | bytes 1769476
  89.7 19.8 %collective-permute-start.18 = (bf16[256,1536]{1,0:T(8,128)(2,1)S(1)}, bf16[256,1536]{1,0:T(8,128)(2,1)S(1)}, u32[]{:S(2)}, u32[]{:S(2)}) collective-permute-start(bf16[256,1536]{1,0:T(8,128)(2,1)S(1)} %get-tuple-element.64.refs_9_.refs_0_), channel_id=1, source_target_pairs={{0,1},{1,0},{2,3},{3,2},{4,5},{5,4},{6,7},{7,6},{8,9},{9,8},{10,11... | collective-permute-start | bytes 2359304 | tf_op jit(solution)/shard_map/ppermute | solution.py:386
  90.9 19.5 %collective-permute-start.19 = (bf16[256,1536]{1,0:T(8,128)(2,1)S(1)}, bf16[256,1536]{1,0:T(8,128)(2,1)S(1)}, u32[]{:S(2)}, u32[]{:S(2)}) collective-permute-start(bf16[256,1536]{1,0:T(8,128)(2,1)S(1)} %get-tuple-element.64.refs_9_.refs_0_), channel_id=1, source_target_pairs={{0,2},{1,3},{2,0},{3,1},{4,6},{5,7},{6,4},{7,5},{8,10},{9,11},{10,... | collective-permute-start | bytes 2359304 | tf_op jit(solution)/shard_map/ppermute | solution.py:386
  95.4 43.9 %copy-start.3 = (bf16[96,3072]{1,0:T(8,128)(2,1)}, bf16[96,3072]{1,0:T(8,128)(2,1)S(1)}, u32[]{:S(2)}) copy-start(bf16[96,3072]{1,0:T(8,128)(2,1)S(1)} %get-tuple-element.106.refs_1_) | copy-start | bytes 1769476
  95.4 43.9 %copy-start.4 = (bf16[96,3072]{1,0:T(8,128)(2,1)}, bf16[96,3072]{1,0:T(8,128)(2,1)S(1)}, u32[]{:S(2)}) copy-start(bf16[96,3072]{1,0:T(8,128)(2,1)S(1)} %get-tuple-element.107.refs_0_) | copy-start | bytes 1769476
  95.4 43.9 %collective-permute-start.16 = (bf16[96,3072]{1,0:T(8,128)(2,1)S(1)}, bf16[96,3072]{1,0:T(8,128)(2,1)S(1)}, u32[]{:S(2)}, u32[]{:S(2)}) collective-permute-start(bf16[96,3072]{1,0:T(8,128)(2,1)S(1)} %get-tuple-element.107.refs_0_), channel_id=1, source_target_pairs={{0,4},{1,5},{2,6},{3,7},{4,0},{5,1},{6,2},{7,3},{8,12},{9,13},{10,... | collective-permute-start | bytes 1769480 | tf_op jit(solution)/shard_map/ppermute | solution.py:386
  95.5 43.8 %collective-permute-start.17 = (bf16[96,3072]{1,0:T(8,128)(2,1)S(1)}, bf16[96,3072]{1,0:T(8,128)(2,1)S(1)}, u32[]{:S(2)}, u32[]{:S(2)}) collective-permute-start(bf16[96,3072]{1,0:T(8,128)(2,1)S(1)} %get-tuple-element.106.refs_1_), channel_id=1, source_target_pairs={{0,4},{1,5},{2,6},{3,7},{4,0},{5,1},{6,2},{7,3},{8,12},{9,13},{10,... | collective-permute-start | bytes 1769480 | tf_op jit(solution)/shard_map/ppermute | solution.py:386
  111.3 13.8 %collective-permute-start.20 = (bf16[128,1536]{1,0:T(8,128)(2,1)}, bf16[128,1536]{1,0:T(8,128)(2,1)S(1)}, u32[]{:S(2)}, u32[]{:S(2)}) collective-permute-start(bf16[128,1536]{1,0:T(8,128)(2,1)} %slice.80), channel_id=1, source_target_pairs={{0,2},{1,3},{2,0},{3,1},{4,6},{5,7},{6,4},{7,5},{8,10},{9,11},{10,... | collective-permute-start | bytes 1179656 | tf_op jit(solution)/shard_map/ppermute | solution.py:386
  113.3 23.1 %collective-permute-start.21 = (bf16[128,1536]{1,0:T(8,128)(2,1)}, bf16[128,1536]{1,0:T(8,128)(2,1)S(1)}, u32[]{:S(2)}, u32[]{:S(2)}) collective-permute-start(bf16[128,1536]{1,0:T(8,128)(2,1)} %slice.81), channel_id=1, source_target_pairs={{0,1},{1,0},{2,3},{3,2},{4,5},{5,4},{6,7},{7,6},{8,9},{9,8},{10,11... | collective-permute-start | bytes 1179656 | tf_op jit(solution)/shard_map/ppermute | solution.py:386
  125.0 23.9 %collective-permute-start.25 = (bf16[48,1536]{1,0:T(8,128)(2,1)}, bf16[48,1536]{1,0:T(8,128)(2,1)}, u32[]{:S(2)}, u32[]{:S(2)}) collective-permute-start(bf16[48,1536]{1,0:T(8,128)(2,1)} %get-tuple-element.104), channel_id=1, source_target_pairs={{0,8},{1,9},{2,10},{3,11},{4,12},{5,13},{6,14},{7,15},{8,16},{9,17... | collective-permute-start | bytes 442376 | tf_op jit(solution)/shard_map/ppermute | solution.py:386
  125.0 14.3 %copy-start.20 = (bf16[128,1536]{1,0:T(8,128)(2,1)}, bf16[128,1536]{1,0:T(8,128)(2,1)S(1)}, u32[]{:S(2)}) copy-start(bf16[128,1536]{1,0:T(8,128)(2,1)S(1)} %collective-permute-done.20.refs_12_.refs_3_) | copy-start | bytes 1179652
  125.0 23.9 %collective-permute-start.26 = (bf16[48,1536]{1,0:T(8,128)(2,1)}, bf16[48,1536]{1,0:T(8,128)(2,1)}, u32[]{:S(2)}, u32[]{:S(2)}) collective-permute-start(bf16[48,1536]{1,0:T(8,128)(2,1)} %get-tuple-element.103), channel_id=1, source_target_pairs={{0,16},{1,17},{2,18},{3,19},{4,20},{5,21},{6,22},{7,23},{8,24},{9,... | collective-permute-start | bytes 442376 | tf_op jit(solution)/shard_map/ppermute | solution.py:386
  136.4 12.6 %collective-permute-start.27 = (bf16[48,1536]{1,0:T(8,128)(2,1)S(1)}, bf16[48,1536]{1,0:T(8,128)(2,1)}, u32[]{:S(2)}, u32[]{:S(2)}) collective-permute-start(bf16[48,1536]{1,0:T(8,128)(2,1)S(1)} %get-tuple-element.102), channel_id=1, source_target_pairs={{0,24},{1,25},{2,26},{3,27},{4,28},{5,29},{6,30},{7,31},{8,0},{9,1... | collective-permute-start | bytes 442376 | tf_op jit(solution)/shard_map/ppermute | solution.py:386
  154.2 16.1 %collective-permute-start.34 = (bf16[4,48,1536]{2,1,0:T(8,128)(2,1)}, bf16[4,48,1536]{2,1,0:T(8,128)(2,1)S(1)}, u32[]{:S(2)}, u32[]{:S(2)}) collective-permute-start(bf16[4,48,1536]{2,1,0:T(8,128)(2,1)} %get-tuple-element.85), channel_id=1, source_target_pairs={{0,4},{1,5},{2,6},{3,7},{4,0},{5,1},{6,2},{7,3},{8,12},{9,13},{10,... | collective-permute-start | bytes 1769480 | tf_op jit(solution)/shard_map/ppermute | solution.py:386
  155.3 15.0 %collective-permute-start.28 = (bf16[48,1536]{1,0:T(8,128)(2,1)S(1)}, bf16[48,1536]{1,0:T(8,128)(2,1)S(1)}, u32[]{:S(2)}, u32[]{:S(2)}) collective-permute-start(bf16[48,1536]{1,0:T(8,128)(2,1)S(1)} %add_convert_fusion.5), channel_id=1, source_target_pairs={{0,1},{1,0},{2,3},{3,2},{4,5},{5,4},{6,7},{7,6},{8,9},{9,8},{10,11... | collective-permute-start | bytes 442376 | tf_op jit(solution)/shard_map/ppermute | solution.py:386
  155.7 14.6 %collective-permute-start.29 = (bf16[48,1536]{1,0:T(8,128)(2,1)S(1)}, bf16[48,1536]{1,0:T(8,128)(2,1)S(1)}, u32[]{:S(2)}, u32[]{:S(2)}) collective-permute-start(bf16[48,1536]{1,0:T(8,128)(2,1)S(1)} %add_convert_fusion.5), channel_id=1, source_target_pairs={{0,2},{1,3},{2,0},{3,1},{4,6},{5,7},{6,4},{7,5},{8,10},{9,11},{10,... | collective-permute-start | bytes 442376 | tf_op jit(solution)/shard_map/ppermute | solution.py:386
  157.3 13.1 %collective-permute-start.30 = (bf16[48,1536]{1,0:T(8,128)(2,1)S(1)}, bf16[48,1536]{1,0:T(8,128)(2,1)S(1)}, u32[]{:S(2)}, u32[]{:S(2)}) collective-permute-start(bf16[48,1536]{1,0:T(8,128)(2,1)S(1)} %add_convert_fusion.5), channel_id=1, source_target_pairs={{0,3},{1,2},{2,1},{3,0},{4,7},{5,6},{6,5},{7,4},{8,11},{9,10},{10,... | collective-permute-start | bytes 442376 | tf_op jit(solution)/shard_map/ppermute | solution.py:386
  158.9 11.5 %copy-start.15 = (bf16[4,48,1536]{2,1,0:T(8,128)(2,1)S(1)}, bf16[4,48,1536]{2,1,0:T(8,128)(2,1)}, u32[]{:S(2)}) copy-start(bf16[4,48,1536]{2,1,0:T(8,128)(2,1)} %get-tuple-element.86) | copy-start | bytes 1769476
  170.4 12.1 %copy-start.30 = (bf16[3,256,384]{2,1,0:T(8,128)(2,1)S(1)}, bf16[3,256,384]{2,1,0:T(8,128)(2,1)}, u32[]{:S(2)}) copy-start(bf16[3,256,384]{2,1,0:T(8,128)(2,1)} %get-tuple-element.68) | copy-start | bytes 1769476
  170.4 13.8 %copy-start.29 = (bf16[3,256,384]{2,1,0:T(8,128)(2,1)S(1)}, bf16[3,256,384]{2,1,0:T(8,128)(2,1)}, u32[]{:S(2)}) copy-start(bf16[3,256,384]{2,1,0:T(8,128)(2,1)} %get-tuple-element.69) | copy-start | bytes 1769476
  170.4 15.6 %copy-start.28 = (bf16[3,256,384]{2,1,0:T(8,128)(2,1)S(1)}, bf16[3,256,384]{2,1,0:T(8,128)(2,1)}, u32[]{:S(2)}) copy-start(bf16[3,256,384]{2,1,0:T(8,128)(2,1)} %get-tuple-element.70) | copy-start | bytes 1769476
  170.5 6.8 %collective-permute-start.35 = (bf16[48,1536]{1,0:T(8,128)(2,1)S(1)}, bf16[48,1536]{1,0:T(8,128)(2,1)S(1)}, u32[]{:S(2)}, u32[]{:S(2)}) collective-permute-start(bf16[48,1536]{1,0:T(8,128)(2,1)S(1)} %get-tuple-element.100), channel_id=1, source_target_pairs={{0,1},{1,0},{2,3},{3,2},{4,5},{5,4},{6,7},{7,6},{8,9},{9,8},{10,11... | collective-permute-start | bytes 442376 | tf_op jit(solution)/shard_map/ppermute | solution.py:386
  170.9 6.5 %collective-permute-start.36 = (bf16[48,1536]{1,0:T(8,128)(2,1)S(1)}, bf16[48,1536]{1,0:T(8,128)(2,1)S(1)}, u32[]{:S(2)}, u32[]{:S(2)}) collective-permute-start(bf16[48,1536]{1,0:T(8,128)(2,1)S(1)} %get-tuple-element.99), channel_id=1, source_target_pairs={{0,2},{1,3},{2,0},{3,1},{4,6},{5,7},{6,4},{7,5},{8,10},{9,11},{10,... | collective-permute-start | bytes 442376 | tf_op jit(solution)/shard_map/ppermute | solution.py:386
  172.5 7.7 %collective-permute-start.37 = (bf16[48,1536]{1,0:T(8,128)(2,1)S(1)}, bf16[48,1536]{1,0:T(8,128)(2,1)S(1)}, u32[]{:S(2)}, u32[]{:S(2)}) collective-permute-start(bf16[48,1536]{1,0:T(8,128)(2,1)S(1)} %get-tuple-element.98), channel_id=1, source_target_pairs={{0,3},{1,2},{2,1},{3,0},{4,7},{5,6},{6,5},{7,4},{8,11},{9,10},{10,... | collective-permute-start | bytes 442376 | tf_op jit(solution)/shard_map/ppermute | solution.py:386
  174.8 9.3 %collective-permute-start.31 = (bf16[48,1536]{1,0:T(8,128)(2,1)S(1)}, bf16[48,1536]{1,0:T(8,128)(2,1)S(1)}, u32[]{:S(2)}, u32[]{:S(2)}) collective-permute-start(bf16[48,1536]{1,0:T(8,128)(2,1)S(1)} %get-tuple-element.115), channel_id=1, source_target_pairs={{0,8},{1,9},{2,10},{3,11},{4,12},{5,13},{6,14},{7,15},{8,16},{9,17... | collective-permute-start | bytes 442376 | tf_op jit(solution)/shard_map/ppermute | solution.py:386
  180.3 5.7 %collective-permute-start.40 = (bf16[48,1536]{1,0:T(8,128)(2,1)S(1)}, bf16[48,1536]{1,0:T(8,128)(2,1)S(1)}, u32[]{:S(2)}, u32[]{:S(2)}) collective-permute-start(bf16[48,1536]{1,0:T(8,128)(2,1)S(1)} %get-tuple-element.111), channel_id=1, source_target_pairs={{0,24},{1,25},{2,26},{3,27},{4,28},{5,29},{6,30},{7,31},{8,0},{9,1... | collective-permute-start | bytes 442376 | tf_op jit(solution)/shard_map/ppermute | solution.py:386
  180.4 13.6 %collective-permute-start.39 = (bf16[48,1536]{1,0:T(8,128)(2,1)S(1)}, bf16[48,1536]{1,0:T(8,128)(2,1)S(1)}, u32[]{:S(2)}, u32[]{:S(2)}) collective-permute-start(bf16[48,1536]{1,0:T(8,128)(2,1)S(1)} %get-tuple-element.112), channel_id=1, source_target_pairs={{0,16},{1,17},{2,18},{3,19},{4,20},{5,21},{6,22},{7,23},{8,24},{9,... | collective-permute-start | bytes 442376 | tf_op jit(solution)/shard_map/ppermute | solution.py:386
  180.6 13.4 %collective-permute-start.38 = (bf16[48,1536]{1,0:T(8,128)(2,1)S(1)}, bf16[48,1536]{1,0:T(8,128)(2,1)S(1)}, u32[]{:S(2)}, u32[]{:S(2)}) collective-permute-start(bf16[48,1536]{1,0:T(8,128)(2,1)S(1)} %get-tuple-element.110), channel_id=1, source_target_pairs={{0,8},{1,9},{2,10},{3,11},{4,12},{5,13},{6,14},{7,15},{8,16},{9,17... | collective-permute-start | bytes 442376 | tf_op jit(solution)/shard_map/ppermute | solution.py:386
  182.5 22.5 %collective-permute-start.22 = (bf16[3,256,384]{2,1,0:T(8,128)(2,1)S(1)}, bf16[3,256,384]{2,1,0:T(8,128)(2,1)S(1)}, u32[]{:S(2)}, u32[]{:S(2)}) collective-permute-start(bf16[3,256,384]{2,1,0:T(8,128)(2,1)S(1)} %copy-done.30), channel_id=1, source_target_pairs={{0,1},{1,0},{2,3},{3,2},{4,5},{5,4},{6,7},{7,6},{8,9},{9,8},{10,11... | collective-permute-start | bytes 1769480 | tf_op jit(solution)/shard_map/ppermute | solution.py:386
  184.2 28.0 %copy-start.22 = (bf16[48,1536]{1,0:T(8,128)(2,1)}, bf16[48,1536]{1,0:T(8,128)(2,1)S(1)}, u32[]{:S(2)}) copy-start(bf16[48,1536]{1,0:T(8,128)(2,1)S(1)} %collective-permute-done.31.refs_5_) | copy-start | bytes 442372
  184.2 24.5 %collective-permute-start.23 = (bf16[3,256,384]{2,1,0:T(8,128)(2,1)S(1)}, bf16[3,256,384]{2,1,0:T(8,128)(2,1)S(1)}, u32[]{:S(2)}, u32[]{:S(2)}) collective-permute-start(bf16[3,256,384]{2,1,0:T(8,128)(2,1)S(1)} %copy-done.29), channel_id=1, source_target_pairs={{0,2},{1,3},{2,0},{3,1},{4,6},{5,7},{6,4},{7,5},{8,10},{9,11},{10,... | collective-permute-start | bytes 1769480 | tf_op jit(solution)/shard_map/ppermute | solution.py:386
  186.0 26.2 %collective-permute-start.24 = (bf16[3,256,384]{2,1,0:T(8,128)(2,1)S(1)}, bf16[3,256,384]{2,1,0:T(8,128)(2,1)S(1)}, u32[]{:S(2)}, u32[]{:S(2)}) collective-permute-start(bf16[3,256,384]{2,1,0:T(8,128)(2,1)S(1)} %copy-done.28), channel_id=1, source_target_pairs={{0,3},{1,2},{2,1},{3,0},{4,7},{5,6},{6,5},{7,4},{8,11},{9,10},{10,... | collective-permute-start | bytes 1769480 | tf_op jit(solution)/shard_map/ppermute | solution.py:386
  194.0 8.6 %collective-permute-start.32 = (bf16[48,1536]{1,0:T(8,128)(2,1)S(1)}, bf16[48,1536]{1,0:T(8,128)(2,1)S(1)}, u32[]{:S(2)}, u32[]{:S(2)}) collective-permute-start(bf16[48,1536]{1,0:T(8,128)(2,1)S(1)} %get-tuple-element.114), channel_id=1, source_target_pairs={{0,16},{1,17},{2,18},{3,19},{4,20},{5,21},{6,22},{7,23},{8,24},{9,... | collective-permute-start | bytes 442376 | tf_op jit(solution)/shard_map/ppermute | solution.py:386
  194.0 8.8 %collective-permute-start.33 = (bf16[48,1536]{1,0:T(8,128)(2,1)S(1)}, bf16[48,1536]{1,0:T(8,128)(2,1)S(1)}, u32[]{:S(2)}, u32[]{:S(2)}) collective-permute-start(bf16[48,1536]{1,0:T(8,128)(2,1)S(1)} %get-tuple-element.113), channel_id=1, source_target_pairs={{0,24},{1,25},{2,26},{3,27},{4,28},{5,29},{6,30},{7,31},{8,0},{9,1... | collective-permute-start | bytes 442376 | tf_op jit(solution)/shard_map/ppermute | solution.py:386
  196.1 21.0 %copy-start.14 = (bf16[48,1536]{1,0:T(8,128)(2,1)}, bf16[48,1536]{1,0:T(8,128)(2,1)S(1)}, u32[]{:S(2)}) copy-start(bf16[48,1536]{1,0:T(8,128)(2,1)S(1)} %add_convert_fusion.refs_0_) | copy-start | bytes 442372
  202.6 9.6 %copy-start.23 = (bf16[48,1536]{1,0:T(8,128)(2,1)}, bf16[48,1536]{1,0:T(8,128)(2,1)S(1)}, u32[]{:S(2)}) copy-start(bf16[48,1536]{1,0:T(8,128)(2,1)S(1)} %collective-permute-done.32.refs_6_) | copy-start | bytes 442372
  202.6 14.5 %collective-permute-start.41 = (bf16[48,1536]{1,0:T(8,128)(2,1)S(1)}, bf16[48,1536]{1,0:T(8,128)(2,1)S(1)}, u32[]{:S(2)}, u32[]{:S(2)}) collective-permute-start(bf16[48,1536]{1,0:T(8,128)(2,1)S(1)} %add_convert_fusion.refs_0_), channel_id=1, source_target_pairs={{0,1},{1,0},{2,3},{3,2},{4,5},{5,4},{6,7},{7,6},{8,9},{9,8},{10,11... | collective-permute-start | bytes 442376 | tf_op jit(solution)/shard_map/ppermute | solution.py:386
  202.8 9.4 %copy-start.24 = (bf16[48,1536]{1,0:T(8,128)(2,1)}, bf16[48,1536]{1,0:T(8,128)(2,1)S(1)}, u32[]{:S(2)}) copy-start(bf16[48,1536]{1,0:T(8,128)(2,1)S(1)} %collective-permute-done.33.refs_7_) | copy-start | bytes 442372
  202.8 14.3 %collective-permute-start.42 = (bf16[48,1536]{1,0:T(8,128)(2,1)S(1)}, bf16[48,1536]{1,0:T(8,128)(2,1)S(1)}, u32[]{:S(2)}, u32[]{:S(2)}) collective-permute-start(bf16[48,1536]{1,0:T(8,128)(2,1)S(1)} %add_convert_fusion.refs_0_), channel_id=1, source_target_pairs={{0,2},{1,3},{2,0},{3,1},{4,6},{5,7},{6,4},{7,5},{8,10},{9,11},{10,... | collective-permute-start | bytes 442376 | tf_op jit(solution)/shard_map/ppermute | solution.py:386
  205.0 7.2 %copy-start.16 = (bf16[3,256,384]{2,1,0:T(8,128)(2,1)}, bf16[3,256,384]{2,1,0:T(8,128)(2,1)S(1)}, u32[]{:S(2)}) copy-start(bf16[3,256,384]{2,1,0:T(8,128)(2,1)S(1)} %collective-permute-done.22.refs_1_) | copy-start | bytes 1769476
  205.0 12.1 %collective-permute-start.43 = (bf16[48,1536]{1,0:T(8,128)(2,1)S(1)}, bf16[48,1536]{1,0:T(8,128)(2,1)S(1)}, u32[]{:S(2)}, u32[]{:S(2)}) collective-permute-start(bf16[48,1536]{1,0:T(8,128)(2,1)S(1)} %add_convert_fusion.refs_0_), channel_id=1, source_target_pairs={{0,3},{1,2},{2,1},{3,0},{4,7},{5,6},{6,5},{7,4},{8,11},{9,10},{10,... | collective-permute-start | bytes 442376 | tf_op jit(solution)/shard_map/ppermute | solution.py:386
  208.7 3.5 %copy-start.17 = (bf16[3,256,384]{2,1,0:T(8,128)(2,1)}, bf16[3,256,384]{2,1,0:T(8,128)(2,1)S(1)}, u32[]{:S(2)}) copy-start(bf16[3,256,384]{2,1,0:T(8,128)(2,1)S(1)} %collective-permute-done.23.refs_2_) | copy-start | bytes 1769476
  (11 other events, 14.5 us)
where the time goes:
time: 221 us
  waiting for transfers between devices  76.9 us (35%)
  starting transfers between devices  73.7 us (33%)
  Pallas kernels  52.4 us (24%)
  other arithmetic  8.35 us (4%)
  local copies, waits for them, and re-layouts  8.07 us (4%)
    ppermute x44, waiting for transfers between devices, send(): return lax.ppermute(array, ('fsdp', 'rows'), pairs)  76.9 us
    ppermute x44, starting transfers between devices, send(): return lax.ppermute(array, ('fsdp', 'rows'), pairs)  73.7 us
    pallas_call x1, Pallas kernels, forward(): pl.pallas_call(body, grid=(heads,), in_specs=[part] * rows, out_specs=[pl...  12.6 us
    pallas_call x1, Pallas kernels, backward(): pl.pallas_call(body, grid=(count,), in_specs=[part] * rows + [pl.BlockSpe...  11.4 us
    pallas_call x2, Pallas kernels, weight_terms(): pl.pallas_call(body, grid_spec=pltpu.PrefetchScalarGridSpec(num_scalar_pr...  10.4 us
    pallas_call x1, Pallas kernels, project(): pl.pallas_call(body, grid_spec=pltpu.PrefetchScalarGridSpec(num_scalar_pr...  8.03 us
  transfers between devices with their start and end apart: 44, of which 14 were waited for; matrix products, arithmetic and copies ran while one was open for 5% of the time, Pallas kernels for 20%

commit v1 on v0

--- a/solution.py
+++ b/solution.py
@@ -271,7 +271,8 @@
 
 
 def project(place, weights, grads):
-    chunks, count = len(grads), len(grads[0])
+    chunks = len(grads)
+    ends = [sum(len(chunk) for chunk in grads[: at + 1]) for at in range(chunks)]
     half, depth = weights[0].shape
     half = half * len(weights) // 2
     step = grads[0][0].shape[1] // 2
@@ -284,7 +285,7 @@
 
             @pl.when(at // 2 == chunk)
             def _():
-                term = dot(lines, stacked(ins[chunk * count : (chunk + 1) * count]), NT)
+                term = dot(lines, stacked(ins[ends[chunk] - len(grads[chunk]) : ends[chunk]]), NT)
                 if chunk:
                     total[...] += term
                 else:
@@ -397,15 +398,19 @@
     grad_flat = grad_out[0]
     wide = grad_flat.shape[1] // 2
 
-    def gather(chunk, *done):
-        by_x, by_y = to_row(chunk, 1), to_row(chunk, 2)
-        by_x, by_y = after((by_x, by_y), *done)
-        cut = chunk.shape[0] // 2
-        upper, lower = by_x[:cut], by_y[cut:]
-        by_both = [to_row(upper, 2), to_row(lower, 1)]
-        return [chunk, by_x, by_y, *by_both]
-
-    grads = [gather(grad_flat[:, :wide])]
+    half_way = grad_flat.shape[0] // 2
+    left, upper, lower = (
+        grad_flat[:, :wide],
+        grad_flat[:half_way, wide:],
+        grad_flat[half_way:, wide:],
+    )
+
+    def hand_on(by_x, by_y):
+        return [to_row(by_x, 2), to_row(by_y, 1)]
+
+    by_x, by_y = to_row(left, 1), to_row(left, 2)
+    handed = by_x[:half_way], by_y[half_way:]
+    grads = [[left, by_x, by_y, *hand_on(*handed)]]
 
     away = jnp.abs(plane - row)
     cut = w_out.shape[0] // 2
@@ -437,7 +442,11 @@
             here = jnp.where(away == hop, stages[hop], here)
         return here
 
-    grads.append(gather(after(grad_flat[:, wide:], parts), attended))
+    own = after((upper, lower), parts)
+    by_x = [to_row(part, 1) for part in own]
+    by_y = [to_row(part, 2) for part in own]
+    by_x, by_y = after((by_x, by_y), attended)
+    grads.append([*own, *by_x, *by_y, *hand_on(by_x[0], by_y[1])])
 
 
     def reduce_cores(at, attended, chunk):
@@ -471,7 +480,7 @@
     first[-1], second[-1] = after((first[-1], second[-1]), early[0])
     weights = [mine(first), mine(second)]
     weights += [to_core(part) for part in weights]
-    late = reduce_cores(1, after(attended, weights), grads[1])
+    late = reduce_cores(1, attended, grads[1])
     grad_attn = project(place, weights, grads)
     late = to_rows(add_cores(*after(late, grad_attn)))
     early = to_rows([added(after(early, grad_attn))] * rows)

time: 221 us -> 214 us (0.968)
  waiting for transfers between devices: 76.9 us -> 66.8 us
  local copies, waits for them, and re-layouts: 8.07 us -> 11.7 us
    ppermute x44 -> x46, waiting for transfers between devices: 76.9 us -> 66.8 us  [send(): return lax.ppermute(array, ('fsdp', 'rows'), pairs)]
    slice x5 -> x4, local copies, waits for them, and re-layouts: 1.76 us -> 4.74 us  [the longest x2 2.64 us: by_heads(): handed = (by_x[:half_way], by_y[half_way:])]
    ppermute x44 -> x46, starting transfers between devices: 73.7 us -> 74.5 us  [send(): return lax.ppermute(array, ('fsdp', 'rows'), pairs)]
  transfers between devices with their start and end apart: 44 -> 46, of which waited for: 14 -> 11; matrix products, arithmetic and copies ran while one was open for 5% -> 5% of each run, Pallas kernels for 20% -> 23%
where the time goes in v1:
time: 214 us; the launch traced here: 213 us
  starting transfers between devices  74.5 us (35%)
  waiting for transfers between devices  66.8 us (31%)
  Pallas kernels  52.5 us (25%)
  local copies, waits for them, and re-layouts  11.7 us (5%)
  other arithmetic  6.5 us (3%)
    ppermute x46, starting transfers between devices, send(): return lax.ppermute(array, ('fsdp', 'rows'), pairs)  74.5 us
    ppermute x46, waiting for transfers between devices, send(): return lax.ppermute(array, ('fsdp', 'rows'), pairs)  66.8 us
    pallas_call x1, Pallas kernels, forward(): pl.pallas_call(body, grid=(heads,), in_specs=[part] * rows, out_specs=[pl...  12.6 us
    pallas_call x1, Pallas kernels, backward(): pl.pallas_call(body, grid=(count,), in_specs=[part] * rows + [pl.BlockSpe...  11.4 us
    pallas_call x2, Pallas kernels, weight_terms(): pl.pallas_call(body, grid_spec=pltpu.PrefetchScalarGridSpec(num_scalar_pr...  10.5 us
    pallas_call x1, Pallas kernels, project(): pl.pallas_call(body, grid_spec=pltpu.PrefetchScalarGridSpec(num_scalar_pr...  8.01 us
    unnamed x62, local copies, waits for them, and re-layouts  5.48 us
  transfers between devices with their start and end apart: 46, of which 11 were waited for; matrix products, arithmetic and copies ran while one was open for 5% of the time, Pallas kernels for 23%

profile of v1, /device:TPU:0, one launch (start us, length us, event | category | flops | bytes accessed | tf_op | source)
XLA Modules:
  0.0 213.1 jit_solution(14743815870740312121)
XLA Ops:
  0.6 1.4 fusion.9
  2.1 5.8 %collective-permute-start.3 = (bf16[96,3072]{1,0:T(8,128)(2,1)S(1)}, bf16[96,3072]{1,0:T(8,128)(2,1)}, u32[]{:S(2)}, u32[]{:S(2)}) collective-permute-start(bf16[96,3072]{1,0:T(8,128)(2,1)S(1)} %get-tuple-element.109), channel_id=1, source_target_pairs={{0,8},{4,12},{9,17},{13,21},{18,26},{22,30}} | collective-permute-start | bytes 1769480 | tf_op jit(solution)/shard_map/ppermute | solution.py:387
  7.9 1.5 collective-permute-start.4
  9.7 9.9 %collective-permute-done.3 = bf16[96,3072]{1,0:T(8,128)(2,1)} collective-permute-done((bf16[96,3072]{1,0:T(8,128)(2,1)S(1)}, bf16[96,3072]{1,0:T(8,128)(2,1)}, u32[]{:S(2)}, u32[]{:S(2)}) %collective-permute-start.3) | collective-permute-done | bytes 589856 | tf_op jit(solution)/shard_map/ppermute | solution.py:387
  19.6 1.1 broadcast_select_fusion.1
  20.8 5.3 %collective-permute-start.7 = (bf16[96,3072]{1,0:T(8,128)(2,1)S(1)}, bf16[96,3072]{1,0:T(8,128)(2,1)}, u32[]{:S(2)}, u32[]{:S(2)}) collective-permute-start(bf16[96,3072]{1,0:T(8,128)(2,1)S(1)} %get-tuple-element.55), channel_id=1, source_target_pairs={{0,8},{4,12},{9,17},{13,21},{18,26},{22,30}} | collective-permute-start | bytes 1769480 | tf_op jit(solution)/shard_map/ppermute | solution.py:387
  26.1 1.5 collective-permute-start.8
  27.5 0.6 pad_add_fusion.place_ref
  28.1 3.3 %pack.1 = (bf16[3,256,384]{2,1,0:T(8,128)(2,1)}, bf16[3,256,384]{2,1,0:T(8,128)(2,1)}, bf16[3,256,384]{2,1,0:T(8,128)(2,1)}, bf16[3,256,384]{2,1,0:T(8,128)(2,1)}) custom-call(s32[3]{0:T(128)} %pad_add_fusion.place_ref, bf16[1,256,1536]{2,1,0:T(8,128)(2,1)} %refs_0_.1, bf16[1,256,1536]{2,1,0:T(8,128)(2,1)} %refs_1_.1, bf16[1,256,1536]{2,1,0:T(8,128)(2,1)} %refs_2_.1), custom_call_target="tpu_custom_call" | custom-call | bytes 4718592 | tf_op jit(solution)/shard_map/pack/pallas_call | solution.py:52
  31.5 1.8 collective-permute-start
  33.3 0.8 slice.93
  34.1 1.7 collective-permute-start.2
  35.8 1.8 slice.94
  37.9 6.3 %collective-permute-start.14 = (bf16[128,1536]{1,0:T(8,128)(2,1)}, bf16[128,1536]{1,0:T(8,128)(2,1)S(1)}, u32[]{:S(2)}, u32[]{:S(2)}) collective-permute-start(bf16[128,1536]{1,0:T(8,128)(2,1)} %slice.94), channel_id=1, source_target_pairs={{0,1},{1,0},{2,3},{3,2},{4,5},{5,4},{6,7},{7,6},{8,9},{9,8},{10,11... | collective-permute-start | bytes 1179656 | tf_op jit(solution)/shard_map/ppermute | solution.py:387
  44.2 1.1 broadcast_select_fusion
  45.3 2.6 %collective-permute-done.refs_1_ = bf16[3,256,384]{2,1,0:T(8,128)(2,1)S(1)} collective-permute-done((bf16[3,256,384]{2,1,0:T(8,128)(2,1)}, bf16[3,256,384]{2,1,0:T(8,128)(2,1)S(1)}, u32[]{:S(2)}, u32[]{:S(2)}) %collective-permute-start) | collective-permute-done | bytes 589856 | tf_op jit(solution)/shard_map/ppermute | solution.py:387
  47.9 0.7 collective-permute-start.5
  48.7 13.6 %collective-permute-done.1.refs_2_ = bf16[3,256,384]{2,1,0:T(8,128)(2,1)S(1)} collective-permute-done((bf16[3,256,384]{2,1,0:T(8,128)(2,1)}, bf16[3,256,384]{2,1,0:T(8,128)(2,1)S(1)}, u32[]{:S(2)}, u32[]{:S(2)}) %collective-permute-start.1) | collective-permute-done | bytes 589856 | tf_op jit(solution)/shard_map/ppermute | solution.py:387
  62.3 0.8 copy-done.27
  63.2 0.7 collective-permute-start.9
  63.9 12.6 %forward.1 = (bf16[3,1024,1024]{2,1,0:T(8,128)(2,1)}, bf16[384,1024]{1,0:T(8,128)(2,1)}) custom-call(bf16[3,256,384]{2,1,0:T(8,128)(2,1)} %get-tuple-element.50.refs_0_, bf16[3,256,384]{2,1,0:T(8,128)(2,1)} %copy-done.26, bf16[3,256,384]{2,1,0:T(8,128)(2,1)} %copy-done.27, bf16[3,256,384]{2,1,0:T(8,128)(2,1)} %collective-permute-done.2.refs_3_), custom_call_target="tpu_custom_call" | custom-call | flops 3221225472 | bytes 6291456 | tf_op jit(solution)/shard_map/forward/pallas_call | solution.py:204
  76.5 0.8 copy-done.16
  77.4 5.2 %weight_terms.2 = (bf16[4,48,1536]{2,1,0:T(8,128)(2,1)}, bf16[4,48,1536]{2,1,0:T(8,128)(2,1)}) custom-call(s32[3]{0:T(128)} %pad_add_fusion.place_ref, bf16[384,1024]{1,0:T(8,128)(2,1)} %get-tuple-element.56.attended_ref, bf16[256,1536]{1,0:T(8,128)(2,1)} %copy-done.1, bf16[256,1536]{1,0:T(8,128)(2,1)} %copy-done.4, ...), custom_call_target="tpu_custom_call" | custom-call | flops 1207959552 | bytes 3932160 | tf_op jit(solution)/shard_map/weight_terms/pallas_call | solution.py:348
  82.7 1.6 collective-permute-start.6
  84.3 1.5 collective-permute-start.10
  85.8 2.0 fusion.8
  88.4 2.0 collective-permute-start.19
  90.5 2.2 %fusion.3 = (bf16[48,1536]{1,0:T(8,128)(2,1)}, bf16[48,1536]{1,0:T(8,128)(2,1)}, bf16[48,1536]{1,0:T(8,128)(2,1)}, bf16[48,1536]{1,0:T(8,128)(2,1)}) fusion(bf16[4,48,1536]{2,1,0:T(8,128)(2,1)} %collective-permute-done.15, bf16[4,48,1536]{2,1,0:T(8,128)(2,1)} %get-tuple-element.58), kind=kLoop, calls=%fused_computation.17 | loop fusion | flops 1179648 | bytes 1769472 | tf_op jit(solution)/shard_map/convert_element_type | solution.py:458
  92.7 1.5 collective-permute-start.21
  94.5 5.6 %collective-permute-done.18.refs_11_.refs_2_ = bf16[128,1536]{1,0:T(8,128)(2,1)} collective-permute-done((bf16[128,1536]{1,0:T(8,128)(2,1)}, bf16[128,1536]{1,0:T(8,128)(2,1)}, u32[]{:S(2)}, u32[]{:S(2)}) %collective-permute-start.18) | collective-permute-done | bytes 393248 | tf_op jit(solution)/shard_map/ppermute | solution.py:387
  100.1 7.8 %collective-permute-done.19.refs_12_.refs_3_ = bf16[128,1536]{1,0:T(8,128)(2,1)} collective-permute-done((bf16[128,1536]{1,0:T(8,128)(2,1)}, bf16[128,1536]{1,0:T(8,128)(2,1)}, u32[]{:S(2)}, u32[]{:S(2)}) %collective-permute-start.19) | collective-permute-done | bytes 393248 | tf_op jit(solution)/shard_map/ppermute | solution.py:387
  107.9 0.6 collective-permute-start.22
  108.5 8.0 %collective-permute-start.23 = (bf16[128,1536]{1,0:T(8,128)(2,1)}, bf16[128,1536]{1,0:T(8,128)(2,1)S(1)}, u32[]{:S(2)}, u32[]{:S(2)}) collective-permute-start(bf16[128,1536]{1,0:T(8,128)(2,1)} %collective-permute-done.21.refs_14_.refs_5_), channel_id=1, source_target_pairs={{0,1},{1,0},{2,3},{3,2},{4,5},{5,4},{6,7},{7,6},{8,9},{9,8},{10,11... | collective-permute-start | bytes 1179656 | tf_op jit(solution)/shard_map/ppermute | solution.py:387
  116.6 2.1 collective-permute-done.22.refs_15_.refs_6_
  118.7 7.2 %collective-permute-done.23.refs_16_.refs_7_ = bf16[128,1536]{1,0:T(8,128)(2,1)S(1)} collective-permute-done((bf16[128,1536]{1,0:T(8,128)(2,1)}, bf16[128,1536]{1,0:T(8,128)(2,1)S(1)}, u32[]{:S(2)}, u32[]{:S(2)}) %collective-permute-start.23) | collective-permute-done | bytes 393248 | tf_op jit(solution)/shard_map/ppermute | solution.py:387
  125.9 0.7 copy-done.19
  126.6 5.3 %weight_terms.3 = (bf16[4,48,1536]{2,1,0:T(8,128)(2,1)}, bf16[4,48,1536]{2,1,0:T(8,128)(2,1)}) custom-call(s32[3]{0:T(128)} %pad_add_fusion.place_ref, bf16[384,1024]{1,0:T(8,128)(2,1)} %get-tuple-element.56.attended_ref, bf16[128,1536]{1,0:T(8,128)(2,1)} %get-tuple-element.62.refs_9_.refs_0_, bf16[128,1536]{1,0:T(8,128)(2,1)} %get-tuple-element.63.refs_10_.refs_1_, ...), custom_call_target="tpu_custom_call" | custom-call | flops 1207959552 | bytes 3932160 | tf_op jit(solution)/shard_map/weight_terms/pallas_call | solution.py:348
  132.1 5.1 %collective-permute-start.28 = (bf16[48,1536]{1,0:T(8,128)(2,1)}, bf16[48,1536]{1,0:T(8,128)(2,1)S(1)}, u32[]{:S(2)}, u32[]{:S(2)}) collective-permute-start(bf16[48,1536]{1,0:T(8,128)(2,1)} %get-tuple-element.103), channel_id=1, source_target_pairs={{0,16},{1,17},{2,18},{3,19},{4,20},{5,21},{6,22},{7,23},{8,24},{9,... | collective-permute-start | bytes 442376 | tf_op jit(solution)/shard_map/ppermute | solution.py:387
  138.1 0.8 copy-done.7
  138.9 8.0 %project.1.refs_5_ = bf16[384,1024]{1,0:T(8,128)(2,1)} custom-call(s32[3]{0:T(128)} %pad_add_fusion.place_ref, bf16[96,3072]{1,0:T(8,128)(2,1)} %copy-done.3, bf16[96,3072]{1,0:T(8,128)(2,1)} %copy-done.2, bf16[96,3072]{1,0:T(8,128)(2,1)} %copy-done.6, bf16[96,3072]{1,0:T(8,128)(2,1)} %copy-done.7, bf16[256,1536]{1,0:T(8,128)(2,1)} %copy-done.1, ...), custom_call_target="tpu_custom_call" | custom-call | flops 2415919104 | bytes 8650752 | tf_op jit(solution)/shard_map/project/pallas_call | solution.py:309
  146.9 0.8 collective-permute-done.28
  148.2 1.4 collective-permute-start.31
  149.6 1.7 collective-permute-start.32
  151.9 1.4 collective-permute-start.38
  153.3 11.4 %backward.1 = (bf16[3,256,384]{2,1,0:T(8,128)(2,1)}, bf16[3,256,384]{2,1,0:T(8,128)(2,1)}, bf16[3,256,384]{2,1,0:T(8,128)(2,1)}, bf16[3,256,384]{2,1,0:T(8,128)(2,1)}) custom-call(bf16[3,256,384]{2,1,0:T(8,128)(2,1)} %get-tuple-element.50.refs_0_, bf16[3,256,384]{2,1,0:T(8,128)(2,1)} %copy-done.26, bf16[3,256,384]{2,1,0:T(8,128)(2,1)} %copy-done.27, ...), custom_call_target="tpu_custom_call" | custom-call | flops 3221225472 | bytes 6291456 | tf_op jit(solution)/shard_map/backward/pallas_call | solution.py:253
  164.8 1.7 collective-permute-start.39
  166.5 0.7 select_select_fusion.5
  167.3 3.7 %collective-permute-start.33 = (bf16[48,1536]{1,0:T(8,128)(2,1)S(1)}, bf16[48,1536]{1,0:T(8,128)(2,1)S(1)}, u32[]{:S(2)}, u32[]{:S(2)}) collective-permute-start(bf16[48,1536]{1,0:T(8,128)(2,1)S(1)} %get-tuple-element.115), channel_id=1, source_target_pairs={{0,8},{1,9},{2,10},{3,11},{4,12},{5,13},{6,14},{7,15},{8,16},{9,17... | collective-permute-start | bytes 442376 | tf_op jit(solution)/shard_map/ppermute | solution.py:387
  171.0 3.2 %collective-permute-start.42 = (bf16[48,1536]{1,0:T(8,128)(2,1)S(1)}, bf16[48,1536]{1,0:T(8,128)(2,1)S(1)}, u32[]{:S(2)}, u32[]{:S(2)}) collective-permute-start(bf16[48,1536]{1,0:T(8,128)(2,1)S(1)} %get-tuple-element.111), channel_id=1, source_target_pairs={{0,24},{1,25},{2,26},{3,27},{4,28},{5,29},{6,30},{7,31},{8,0},{9,1... | collective-permute-start | bytes 442376 | tf_op jit(solution)/shard_map/ppermute | solution.py:387
  174.2 1.7 collective-permute-start.41
  175.9 1.5 collective-permute-start.24
  177.4 1.1 collective-permute-start.25
  178.5 2.6 %collective-permute-start.26 = (bf16[3,256,384]{2,1,0:T(8,128)(2,1)S(1)}, bf16[3,256,384]{2,1,0:T(8,128)(2,1)S(1)}, u32[]{:S(2)}, u32[]{:S(2)}) collective-permute-start(bf16[3,256,384]{2,1,0:T(8,128)(2,1)S(1)} %copy-done.28), channel_id=1, source_target_pairs={{0,3},{1,2},{2,1},{3,0},{4,7},{5,6},{6,5},{7,4},{8,11},{9,10},{10,... | collective-permute-start | bytes 1769480 | tf_op jit(solution)/shard_map/ppermute | solution.py:387
  181.0 7.8 %collective-permute-done.41 = bf16[48,1536]{1,0:T(8,128)(2,1)S(1)} collective-permute-done((bf16[48,1536]{1,0:T(8,128)(2,1)S(1)}, bf16[48,1536]{1,0:T(8,128)(2,1)S(1)}, u32[]{:S(2)}, u32[]{:S(2)}) %collective-permute-start.41) | collective-permute-done | bytes 147488 | tf_op jit(solution)/shard_map/ppermute | solution.py:387
  188.9 2.6 %collective-permute-start.35 = (bf16[48,1536]{1,0:T(8,128)(2,1)S(1)}, bf16[48,1536]{1,0:T(8,128)(2,1)S(1)}, u32[]{:S(2)}, u32[]{:S(2)}) collective-permute-start(bf16[48,1536]{1,0:T(8,128)(2,1)S(1)} %get-tuple-element.113), channel_id=1, source_target_pairs={{0,24},{1,25},{2,26},{3,27},{4,28},{5,29},{6,30},{7,31},{8,0},{9,1... | collective-permute-start | bytes 442376 | tf_op jit(solution)/shard_map/ppermute | solution.py:387
  191.6 5.3 %collective-permute-done.34.refs_6_ = bf16[48,1536]{1,0:T(8,128)(2,1)S(1)} collective-permute-done((bf16[48,1536]{1,0:T(8,128)(2,1)S(1)}, bf16[48,1536]{1,0:T(8,128)(2,1)S(1)}, u32[]{:S(2)}, u32[]{:S(2)}) %collective-permute-start.34) | collective-permute-done | bytes 147488 | tf_op jit(solution)/shard_map/ppermute | solution.py:387
  197.0 0.6 collective-permute-start.43
  197.5 1.0 collective-permute-start.44
  198.6 1.9 collective-permute-start.45
  200.5 4.0 %collective-permute-done.25.refs_2_ = bf16[3,256,384]{2,1,0:T(8,128)(2,1)S(1)} collective-permute-done((bf16[3,256,384]{2,1,0:T(8,128)(2,1)S(1)}, bf16[3,256,384]{2,1,0:T(8,128)(2,1)S(1)}, u32[]{:S(2)}, u32[]{:S(2)}) %collective-permute-start.25) | collective-permute-done | bytes 589856 | tf_op jit(solution)/shard_map/ppermute | solution.py:387
  204.5 0.8 copy-done.14
  205.4 4.0 %finish.1 = (bf16[1,256,1536]{2,1,0:T(8,128)(2,1)}, bf16[1,256,1536]{2,1,0:T(8,128)(2,1)}, bf16[1,256,1536]{2,1,0:T(8,128)(2,1)}, f32[192,3072]{1,0:T(8,128)}) custom-call(s32[3]{0:T(128)} %pad_add_fusion.place_ref, bf16[3,256,384]{2,1,0:T(8,128)(2,1)} %get-tuple-element.68.refs_0_, bf16[3,256,384]{2,1,0:T(8,128)(2,1)} %copy-done.13, ...), custom_call_target="tpu_custom_call" | custom-call | bytes 6488064 | tf_op jit(solution)/shard_map/finish/pallas_call | solution.py:133
  209.5 0.6 copy-done.23
  210.3 2.7 %finish_terms.1 = f32[192,3072]{1,0:T(8,128)} custom-call(s32[3]{0:T(128)} %pad_add_fusion.place_ref, f32[192,3072]{1,0:T(8,128)} %get-tuple-element.83._, bf16[48,1536]{1,0:T(8,128)(2,1)} %copy-done.10, bf16[48,1536]{1,0:T(8,128)(2,1)} %copy-done.23, bf16[48,1536]{1,0:T(8,128)(2,1)} %copy-done.24, ...), custom_call_target="tpu_custom_call", output_to_operand_aliasing={{}: (1, {})} | custom-call | bytes 1769472 | tf_op jit(solution)/shard_map/finish_terms/pallas_call | solution.py:163
  (113 shorter events, 4.6 us)
Async XLA Ops:
  0.6 8.7 %copy-start.5 = (bf16[1,256,3072]{2,1,0:T(8,128)(2,1)S(1)}, bf16[1,256,3072]{2,1,0:T(8,128)(2,1)}, u32[]{:S(2)}) copy-start(bf16[1,256,3072]{2,1,0:T(8,128)(2,1)} %param.8) | copy-start | bytes 4718596
  2.1 17.5 %collective-permute-start.3 = (bf16[96,3072]{1,0:T(8,128)(2,1)S(1)}, bf16[96,3072]{1,0:T(8,128)(2,1)}, u32[]{:S(2)}, u32[]{:S(2)}) collective-permute-start(bf16[96,3072]{1,0:T(8,128)(2,1)S(1)} %get-tuple-element.109), channel_id=1, source_target_pairs={{0,8},{4,12},{9,17},{13,21},{18,26},{22,30}} | collective-permute-start | bytes 1769480 | tf_op jit(solution)/shard_map/ppermute | solution.py:387
  7.9 11.7 %collective-permute-start.4 = (bf16[96,3072]{1,0:T(8,128)(2,1)S(1)}, bf16[96,3072]{1,0:T(8,128)(2,1)}, u32[]{:S(2)}, u32[]{:S(2)}) collective-permute-start(bf16[96,3072]{1,0:T(8,128)(2,1)S(1)} %get-tuple-element.109), channel_id=1, source_target_pairs={{9,1},{13,5},{18,10},{22,14},{27,19},{31,23}} | collective-permute-start | bytes 1769480 | tf_op jit(solution)/shard_map/ppermute | solution.py:387
  9.4 22.0 %copy-start.1 = (bf16[256,1536]{1,0:T(8,128)(2,1)}, bf16[256,1536]{1,0:T(8,128)(2,1)S(1)}, u32[]{:S(2)}) copy-start(bf16[256,1536]{1,0:T(8,128)(2,1)S(1)} %slice.92.refs_0_.refs_4_) | copy-start | bytes 2359300
  9.4 23.8 %collective-permute-start.11 = (bf16[256,1536]{1,0:T(8,128)(2,1)S(1)}, bf16[256,1536]{1,0:T(8,128)(2,1)S(1)}, u32[]{:S(2)}, u32[]{:S(2)}) collective-permute-start(bf16[256,1536]{1,0:T(8,128)(2,1)S(1)} %slice.92.refs_0_.refs_4_), channel_id=1, source_target_pairs={{0,1},{1,0},{2,3},{3,2},{4,5},{5,4},{6,7},{7,6},{8,9},{9,8},{10,11... | collective-permute-start | bytes 2359304 | tf_op jit(solution)/shard_map/ppermute | solution.py:387
  9.5 24.6 %collective-permute-start.12 = (bf16[256,1536]{1,0:T(8,128)(2,1)S(1)}, bf16[256,1536]{1,0:T(8,128)(2,1)}, u32[]{:S(2)}, u32[]{:S(2)}) collective-permute-start(bf16[256,1536]{1,0:T(8,128)(2,1)S(1)} %slice.92.refs_0_.refs_4_), channel_id=1, source_target_pairs={{0,2},{1,3},{2,0},{3,1},{4,6},{5,7},{6,4},{7,5},{8,10},{9,11},{10,... | collective-permute-start | bytes 2359304 | tf_op jit(solution)/shard_map/ppermute | solution.py:387
  20.8 16.9 %collective-permute-start.7 = (bf16[96,3072]{1,0:T(8,128)(2,1)S(1)}, bf16[96,3072]{1,0:T(8,128)(2,1)}, u32[]{:S(2)}, u32[]{:S(2)}) collective-permute-start(bf16[96,3072]{1,0:T(8,128)(2,1)S(1)} %get-tuple-element.55), channel_id=1, source_target_pairs={{0,8},{4,12},{9,17},{13,21},{18,26},{22,30}} | collective-permute-start | bytes 1769480 | tf_op jit(solution)/shard_map/ppermute | solution.py:387
  26.1 11.8 %collective-permute-start.8 = (bf16[96,3072]{1,0:T(8,128)(2,1)S(1)}, bf16[96,3072]{1,0:T(8,128)(2,1)}, u32[]{:S(2)}, u32[]{:S(2)}) collective-permute-start(bf16[96,3072]{1,0:T(8,128)(2,1)S(1)} %get-tuple-element.55), channel_id=1, source_target_pairs={{9,1},{13,5},{18,10},{22,14},{27,19},{31,23}} | collective-permute-start | bytes 1769480 | tf_op jit(solution)/shard_map/ppermute | solution.py:387
  31.5 16.5 %collective-permute-start = (bf16[3,256,384]{2,1,0:T(8,128)(2,1)}, bf16[3,256,384]{2,1,0:T(8,128)(2,1)S(1)}, u32[]{:S(2)}, u32[]{:S(2)}) collective-permute-start(bf16[3,256,384]{2,1,0:T(8,128)(2,1)} %get-tuple-element.51), channel_id=1, source_target_pairs={{0,1},{1,0},{2,3},{3,2},{4,5},{5,4},{6,7},{7,6},{8,9},{9,8},{10,11... | collective-permute-start | bytes 1769480 | tf_op jit(solution)/shard_map/ppermute | solution.py:387
  33.3 12.1 %copy-start.4 = (bf16[256,1536]{1,0:T(8,128)(2,1)}, bf16[256,1536]{1,0:T(8,128)(2,1)S(1)}, u32[]{:S(2)}) copy-start(bf16[256,1536]{1,0:T(8,128)(2,1)S(1)} %collective-permute-done.11.refs_1_.refs_5_) | copy-start | bytes 2359300
  33.3 29.0 %collective-permute-start.1 = (bf16[3,256,384]{2,1,0:T(8,128)(2,1)}, bf16[3,256,384]{2,1,0:T(8,128)(2,1)S(1)}, u32[]{:S(2)}, u32[]{:S(2)}) collective-permute-start(bf16[3,256,384]{2,1,0:T(8,128)(2,1)} %get-tuple-element.52), channel_id=1, source_target_pairs={{0,2},{1,3},{2,0},{3,1},{4,6},{5,7},{6,4},{7,5},{8,10},{9,11},{10,... | collective-permute-start | bytes 1769480 | tf_op jit(solution)/shard_map/ppermute | solution.py:387
  34.1 29.7 %collective-permute-start.2 = (bf16[3,256,384]{2,1,0:T(8,128)(2,1)}, bf16[3,256,384]{2,1,0:T(8,128)(2,1)}, u32[]{:S(2)}, u32[]{:S(2)}) collective-permute-start(bf16[3,256,384]{2,1,0:T(8,128)(2,1)} %get-tuple-element.53), channel_id=1, source_target_pairs={{0,3},{1,2},{2,1},{3,0},{4,7},{5,6},{6,5},{7,4},{8,11},{9,10},{10,... | collective-permute-start | bytes 1769480 | tf_op jit(solution)/shard_map/ppermute | solution.py:387
  37.6 38.8 %collective-permute-start.13 = (bf16[128,1536]{1,0:T(8,128)(2,1)}, bf16[128,1536]{1,0:T(8,128)(2,1)S(1)}, u32[]{:S(2)}, u32[]{:S(2)}) collective-permute-start(bf16[128,1536]{1,0:T(8,128)(2,1)} %slice.93), channel_id=1, source_target_pairs={{0,2},{1,3},{2,0},{3,1},{4,6},{5,7},{6,4},{7,5},{8,10},{9,11},{10,... | collective-permute-start | bytes 1179656 | tf_op jit(solution)/shard_map/ppermute | solution.py:387
  37.9 38.5 %collective-permute-start.14 = (bf16[128,1536]{1,0:T(8,128)(2,1)}, bf16[128,1536]{1,0:T(8,128)(2,1)S(1)}, u32[]{:S(2)}, u32[]{:S(2)}) collective-permute-start(bf16[128,1536]{1,0:T(8,128)(2,1)} %slice.94), channel_id=1, source_target_pairs={{0,1},{1,0},{2,3},{3,2},{4,5},{5,4},{6,7},{7,6},{8,9},{9,8},{10,11... | collective-permute-start | bytes 1179656 | tf_op jit(solution)/shard_map/ppermute | solution.py:387
  47.9 34.7 %collective-permute-start.5 = (bf16[96,3072]{1,0:T(8,128)(2,1)S(1)}, bf16[96,3072]{1,0:T(8,128)(2,1)S(1)}, u32[]{:S(2)}, u32[]{:S(2)}) collective-permute-start(bf16[96,3072]{1,0:T(8,128)(2,1)S(1)} %broadcast_select_fusion.1), channel_id=1, source_target_pairs={{8,16},{10,2},{12,20},{14,6},{17,25},{19,11},{21,29},{23,15}} | collective-permute-start | bytes 1769480 | tf_op jit(solution)/shard_map/ppermute | solution.py:387
  63.2 21.2 %collective-permute-start.9 = (bf16[96,3072]{1,0:T(8,128)(2,1)S(1)}, bf16[96,3072]{1,0:T(8,128)(2,1)S(1)}, u32[]{:S(2)}, u32[]{:S(2)}) collective-permute-start(bf16[96,3072]{1,0:T(8,128)(2,1)S(1)} %broadcast_select_fusion), channel_id=1, source_target_pairs={{8,16},{10,2},{12,20},{14,6},{17,25},{19,11},{21,29},{23,15}} | collective-permute-start | bytes 1769480 | tf_op jit(solution)/shard_map/ppermute | solution.py:387
  82.6 11.6 %copy-start = (bf16[192,3072]{1,0:T(8,128)(2,1)S(1)}, bf16[192,3072]{1,0:T(8,128)(2,1)}, u32[]{:S(2)}) copy-start(bf16[192,3072]{1,0:T(8,128)(2,1)} %param.9) | copy-start | bytes 3538948
  82.6 5.8 %collective-permute-start.15 = (bf16[4,48,1536]{2,1,0:T(8,128)(2,1)}, bf16[4,48,1536]{2,1,0:T(8,128)(2,1)}, u32[]{:S(2)}, u32[]{:S(2)}) collective-permute-start(bf16[4,48,1536]{2,1,0:T(8,128)(2,1)} %get-tuple-element.59), channel_id=1, source_target_pairs={{0,4},{1,5},{2,6},{3,7},{4,0},{5,1},{6,2},{7,3},{8,12},{9,13},{10,... | collective-permute-start | bytes 1769480 | tf_op jit(solution)/shard_map/ppermute | solution.py:387
  82.7 11.5 %copy-start.8 = (bf16[96,3072]{1,0:T(8,128)(2,1)}, bf16[96,3072]{1,0:T(8,128)(2,1)S(1)}, u32[]{:S(2)}) copy-start(bf16[96,3072]{1,0:T(8,128)(2,1)S(1)} %collective-permute-done.5) | copy-start | bytes 1769476
  82.7 10.0 %collective-permute-start.6 = (bf16[96,3072]{1,0:T(8,128)(2,1)S(1)}, bf16[96,3072]{1,0:T(8,128)(2,1)}, u32[]{:S(2)}, u32[]{:S(2)}) collective-permute-start(bf16[96,3072]{1,0:T(8,128)(2,1)S(1)} %collective-permute-done.5), channel_id=1, source_target_pairs={{11,3},{15,7},{16,24},{20,28}} | collective-permute-start | bytes 1769480 | tf_op jit(solution)/shard_map/ppermute | solution.py:387
  84.3 9.9 %copy-start.9 = (bf16[96,3072]{1,0:T(8,128)(2,1)}, bf16[96,3072]{1,0:T(8,128)(2,1)S(1)}, u32[]{:S(2)}) copy-start(bf16[96,3072]{1,0:T(8,128)(2,1)S(1)} %collective-permute-done.9) | copy-start | bytes 1769476
  84.3 9.9 %collective-permute-start.10 = (bf16[96,3072]{1,0:T(8,128)(2,1)S(1)}, bf16[96,3072]{1,0:T(8,128)(2,1)}, u32[]{:S(2)}, u32[]{:S(2)}) collective-permute-start(bf16[96,3072]{1,0:T(8,128)(2,1)S(1)} %collective-permute-done.9), channel_id=1, source_target_pairs={{11,3},{15,7},{16,24},{20,28}} | collective-permute-start | bytes 1769480 | tf_op jit(solution)/shard_map/ppermute | solution.py:387
  87.8 12.3 %collective-permute-start.18 = (bf16[128,1536]{1,0:T(8,128)(2,1)}, bf16[128,1536]{1,0:T(8,128)(2,1)}, u32[]{:S(2)}, u32[]{:S(2)}) collective-permute-start(bf16[128,1536]{1,0:T(8,128)(2,1)} %get-tuple-element.62.refs_9_.refs_0_), channel_id=1, source_target_pairs={{0,1},{1,0},{2,3},{3,2},{4,5},{5,4},{6,7},{7,6},{8,9},{9,8},{10,11... | collective-permute-start | bytes 1179656 | tf_op jit(solution)/shard_map/ppermute | solution.py:387
  88.1 19.8 %collective-permute-start.20 = (bf16[128,1536]{1,0:T(8,128)(2,1)}, bf16[128,1536]{1,0:T(8,128)(2,1)}, u32[]{:S(2)}, u32[]{:S(2)}) collective-permute-start(bf16[128,1536]{1,0:T(8,128)(2,1)} %get-tuple-element.62.refs_9_.refs_0_), channel_id=1, source_target_pairs={{0,2},{1,3},{2,0},{3,1},{4,6},{5,7},{6,4},{7,5},{8,10},{9,11},{10,... | collective-permute-start | bytes 1179656 | tf_op jit(solution)/shard_map/ppermute | solution.py:387
  88.4 19.5 %collective-permute-start.19 = (bf16[128,1536]{1,0:T(8,128)(2,1)}, bf16[128,1536]{1,0:T(8,128)(2,1)}, u32[]{:S(2)}, u32[]{:S(2)}) collective-permute-start(bf16[128,1536]{1,0:T(8,128)(2,1)} %get-tuple-element.63.refs_10_.refs_1_), channel_id=1, source_target_pairs={{0,1},{1,0},{2,3},{3,2},{4,5},{5,4},{6,7},{7,6},{8,9},{9,8},{10,11... | collective-permute-start | bytes 1179656 | tf_op jit(solution)/shard_map/ppermute | solution.py:387
  92.7 15.2 %collective-permute-start.21 = (bf16[128,1536]{1,0:T(8,128)(2,1)}, bf16[128,1536]{1,0:T(8,128)(2,1)}, u32[]{:S(2)}, u32[]{:S(2)}) collective-permute-start(bf16[128,1536]{1,0:T(8,128)(2,1)} %get-tuple-element.63.refs_10_.refs_1_), channel_id=1, source_target_pairs={{0,2},{1,3},{2,0},{3,1},{4,6},{5,7},{6,4},{7,5},{8,10},{9,11},{10,... | collective-permute-start | bytes 1179656 | tf_op jit(solution)/shard_map/ppermute | solution.py:387
  94.4 37.5 %copy-start.2 = (bf16[96,3072]{1,0:T(8,128)(2,1)}, bf16[96,3072]{1,0:T(8,128)(2,1)S(1)}, u32[]{:S(2)}) copy-start(bf16[96,3072]{1,0:T(8,128)(2,1)S(1)} %get-tuple-element.106.refs_1_) | copy-start | bytes 1769476
  94.4 37.5 %copy-start.3 = (bf16[96,3072]{1,0:T(8,128)(2,1)}, bf16[96,3072]{1,0:T(8,128)(2,1)S(1)}, u32[]{:S(2)}) copy-start(bf16[96,3072]{1,0:T(8,128)(2,1)S(1)} %get-tuple-element.107.refs_0_) | copy-start | bytes 1769476
  94.5 42.8 %collective-permute-start.16 = (bf16[96,3072]{1,0:T(8,128)(2,1)S(1)}, bf16[96,3072]{1,0:T(8,128)(2,1)S(1)}, u32[]{:S(2)}, u32[]{:S(2)}) collective-permute-start(bf16[96,3072]{1,0:T(8,128)(2,1)S(1)} %get-tuple-element.107.refs_0_), channel_id=1, source_target_pairs={{0,4},{1,5},{2,6},{3,7},{4,0},{5,1},{6,2},{7,3},{8,12},{9,13},{10,... | collective-permute-start | bytes 1769480 | tf_op jit(solution)/shard_map/ppermute | solution.py:387
  100.1 37.6 %collective-permute-start.17 = (bf16[96,3072]{1,0:T(8,128)(2,1)S(1)}, bf16[96,3072]{1,0:T(8,128)(2,1)S(1)}, u32[]{:S(2)}, u32[]{:S(2)}) collective-permute-start(bf16[96,3072]{1,0:T(8,128)(2,1)S(1)} %get-tuple-element.106.refs_1_), channel_id=1, source_target_pairs={{0,4},{1,5},{2,6},{3,7},{4,0},{5,1},{6,2},{7,3},{8,12},{9,13},{10,... | collective-permute-start | bytes 1769480 | tf_op jit(solution)/shard_map/ppermute | solution.py:387
  107.9 10.7 %collective-permute-start.22 = (bf16[128,1536]{1,0:T(8,128)(2,1)}, bf16[128,1536]{1,0:T(8,128)(2,1)S(1)}, u32[]{:S(2)}, u32[]{:S(2)}) collective-permute-start(bf16[128,1536]{1,0:T(8,128)(2,1)} %collective-permute-done.18.refs_11_.refs_2_), channel_id=1, source_target_pairs={{0,2},{1,3},{2,0},{3,1},{4,6},{5,7},{6,4},{7,5},{8,10},{9,11},{10,... | collective-permute-start | bytes 1179656 | tf_op jit(solution)/shard_map/ppermute | solution.py:387
  108.5 17.3 %collective-permute-start.23 = (bf16[128,1536]{1,0:T(8,128)(2,1)}, bf16[128,1536]{1,0:T(8,128)(2,1)S(1)}, u32[]{:S(2)}, u32[]{:S(2)}) collective-permute-start(bf16[128,1536]{1,0:T(8,128)(2,1)} %collective-permute-done.21.refs_14_.refs_5_), channel_id=1, source_target_pairs={{0,1},{1,0},{2,3},{3,2},{4,5},{5,4},{6,7},{7,6},{8,9},{9,8},{10,11... | collective-permute-start | bytes 1179656 | tf_op jit(solution)/shard_map/ppermute | solution.py:387
  118.7 7.2 %copy-start.18 = (bf16[128,1536]{1,0:T(8,128)(2,1)}, bf16[128,1536]{1,0:T(8,128)(2,1)S(1)}, u32[]{:S(2)}) copy-start(bf16[128,1536]{1,0:T(8,128)(2,1)S(1)} %collective-permute-done.22.refs_15_.refs_6_) | copy-start | bytes 1179652
  131.9 19.4 %collective-permute-start.36 = (bf16[4,48,1536]{2,1,0:T(8,128)(2,1)}, bf16[4,48,1536]{2,1,0:T(8,128)(2,1)S(1)}, u32[]{:S(2)}, u32[]{:S(2)}) collective-permute-start(bf16[4,48,1536]{2,1,0:T(8,128)(2,1)} %get-tuple-element.85), channel_id=1, source_target_pairs={{0,4},{1,5},{2,6},{3,7},{4,0},{5,1},{6,2},{7,3},{8,12},{9,13},{10,... | collective-permute-start | bytes 1769480 | tf_op jit(solution)/shard_map/ppermute | solution.py:387
  132.0 14.9 %collective-permute-start.27 = (bf16[48,1536]{1,0:T(8,128)(2,1)}, bf16[48,1536]{1,0:T(8,128)(2,1)S(1)}, u32[]{:S(2)}, u32[]{:S(2)}) collective-permute-start(bf16[48,1536]{1,0:T(8,128)(2,1)} %get-tuple-element.104), channel_id=1, source_target_pairs={{0,8},{1,9},{2,10},{3,11},{4,12},{5,13},{6,14},{7,15},{8,16},{9,17... | collective-permute-start | bytes 442376 | tf_op jit(solution)/shard_map/ppermute | solution.py:387
  132.1 15.6 %collective-permute-start.28 = (bf16[48,1536]{1,0:T(8,128)(2,1)}, bf16[48,1536]{1,0:T(8,128)(2,1)S(1)}, u32[]{:S(2)}, u32[]{:S(2)}) collective-permute-start(bf16[48,1536]{1,0:T(8,128)(2,1)} %get-tuple-element.103), channel_id=1, source_target_pairs={{0,16},{1,17},{2,18},{3,19},{4,20},{5,21},{6,22},{7,23},{8,24},{9,... | collective-permute-start | bytes 442376 | tf_op jit(solution)/shard_map/ppermute | solution.py:387
  137.2 10.5 %copy-start.12 = (bf16[48,1536]{1,0:T(8,128)(2,1)S(1)}, bf16[48,1536]{1,0:T(8,128)(2,1)}, u32[]{:S(2)}) copy-start(bf16[48,1536]{1,0:T(8,128)(2,1)} %get-tuple-element.72) | copy-start | bytes 442372
  137.2 14.1 %copy-start.11 = (bf16[4,48,1536]{2,1,0:T(8,128)(2,1)S(1)}, bf16[4,48,1536]{2,1,0:T(8,128)(2,1)}, u32[]{:S(2)}) copy-start(bf16[4,48,1536]{2,1,0:T(8,128)(2,1)} %get-tuple-element.86) | copy-start | bytes 1769476
  137.2 10.5 %collective-permute-start.29 = (bf16[48,1536]{1,0:T(8,128)(2,1)}, bf16[48,1536]{1,0:T(8,128)(2,1)S(1)}, u32[]{:S(2)}, u32[]{:S(2)}) collective-permute-start(bf16[48,1536]{1,0:T(8,128)(2,1)} %get-tuple-element.102), channel_id=1, source_target_pairs={{0,24},{1,25},{2,26},{3,27},{4,28},{5,29},{6,30},{7,31},{8,0},{9,1... | collective-permute-start | bytes 442376 | tf_op jit(solution)/shard_map/ppermute | solution.py:387
  147.8 17.0 %collective-permute-start.30 = (bf16[48,1536]{1,0:T(8,128)(2,1)S(1)}, bf16[48,1536]{1,0:T(8,128)(2,1)S(1)}, u32[]{:S(2)}, u32[]{:S(2)}) collective-permute-start(bf16[48,1536]{1,0:T(8,128)(2,1)S(1)} %add_convert_fusion.5), channel_id=1, source_target_pairs={{0,1},{1,0},{2,3},{3,2},{4,5},{5,4},{6,7},{7,6},{8,9},{9,8},{10,11... | collective-permute-start | bytes 442376 | tf_op jit(solution)/shard_map/ppermute | solution.py:387
  148.2 18.3 %collective-permute-start.31 = (bf16[48,1536]{1,0:T(8,128)(2,1)S(1)}, bf16[48,1536]{1,0:T(8,128)(2,1)S(1)}, u32[]{:S(2)}, u32[]{:S(2)}) collective-permute-start(bf16[48,1536]{1,0:T(8,128)(2,1)S(1)} %add_convert_fusion.5), channel_id=1, source_target_pairs={{0,2},{1,3},{2,0},{3,1},{4,6},{5,7},{6,4},{7,5},{8,10},{9,11},{10,... | collective-permute-start | bytes 442376 | tf_op jit(solution)/shard_map/ppermute | solution.py:387
  149.6 16.9 %collective-permute-start.32 = (bf16[48,1536]{1,0:T(8,128)(2,1)S(1)}, bf16[48,1536]{1,0:T(8,128)(2,1)S(1)}, u32[]{:S(2)}, u32[]{:S(2)}) collective-permute-start(bf16[48,1536]{1,0:T(8,128)(2,1)S(1)} %add_convert_fusion.5), channel_id=1, source_target_pairs={{0,3},{1,2},{2,1},{3,0},{4,7},{5,6},{6,5},{7,4},{8,11},{9,10},{10,... | collective-permute-start | bytes 442376 | tf_op jit(solution)/shard_map/ppermute | solution.py:387
  151.5 19.5 %collective-permute-start.37 = (bf16[48,1536]{1,0:T(8,128)(2,1)S(1)}, bf16[48,1536]{1,0:T(8,128)(2,1)S(1)}, u32[]{:S(2)}, u32[]{:S(2)}) collective-permute-start(bf16[48,1536]{1,0:T(8,128)(2,1)S(1)} %get-tuple-element.100), channel_id=1, source_target_pairs={{0,1},{1,0},{2,3},{3,2},{4,5},{5,4},{6,7},{7,6},{8,9},{9,8},{10,11... | collective-permute-start | bytes 442376 | tf_op jit(solution)/shard_map/ppermute | solution.py:387
  151.9 19.0 %collective-permute-start.38 = (bf16[48,1536]{1,0:T(8,128)(2,1)S(1)}, bf16[48,1536]{1,0:T(8,128)(2,1)S(1)}, u32[]{:S(2)}, u32[]{:S(2)}) collective-permute-start(bf16[48,1536]{1,0:T(8,128)(2,1)S(1)} %get-tuple-element.99), channel_id=1, source_target_pairs={{0,2},{1,3},{2,0},{3,1},{4,6},{5,7},{6,4},{7,5},{8,10},{9,11},{10,... | collective-permute-start | bytes 442376 | tf_op jit(solution)/shard_map/ppermute | solution.py:387
  164.7 11.2 %copy-start.30 = (bf16[3,256,384]{2,1,0:T(8,128)(2,1)S(1)}, bf16[3,256,384]{2,1,0:T(8,128)(2,1)}, u32[]{:S(2)}) copy-start(bf16[3,256,384]{2,1,0:T(8,128)(2,1)} %get-tuple-element.69) | copy-start | bytes 1769476
  164.7 12.6 %copy-start.29 = (bf16[3,256,384]{2,1,0:T(8,128)(2,1)S(1)}, bf16[3,256,384]{2,1,0:T(8,128)(2,1)}, u32[]{:S(2)}) copy-start(bf16[3,256,384]{2,1,0:T(8,128)(2,1)} %get-tuple-element.70) | copy-start | bytes 1769476
  164.7 13.7 %copy-start.28 = (bf16[3,256,384]{2,1,0:T(8,128)(2,1)S(1)}, bf16[3,256,384]{2,1,0:T(8,128)(2,1)}, u32[]{:S(2)}) copy-start(bf16[3,256,384]{2,1,0:T(8,128)(2,1)} %get-tuple-element.71) | copy-start | bytes 1769476
  164.8 6.2 %collective-permute-start.39 = (bf16[48,1536]{1,0:T(8,128)(2,1)S(1)}, bf16[48,1536]{1,0:T(8,128)(2,1)S(1)}, u32[]{:S(2)}, u32[]{:S(2)}) collective-permute-start(bf16[48,1536]{1,0:T(8,128)(2,1)S(1)} %get-tuple-element.98), channel_id=1, source_target_pairs={{0,3},{1,2},{2,1},{3,0},{4,7},{5,6},{6,5},{7,4},{8,11},{9,10},{10,... | collective-permute-start | bytes 442376 | tf_op jit(solution)/shard_map/ppermute | solution.py:387
  167.3 10.1 %collective-permute-start.33 = (bf16[48,1536]{1,0:T(8,128)(2,1)S(1)}, bf16[48,1536]{1,0:T(8,128)(2,1)S(1)}, u32[]{:S(2)}, u32[]{:S(2)}) collective-permute-start(bf16[48,1536]{1,0:T(8,128)(2,1)S(1)} %get-tuple-element.115), channel_id=1, source_target_pairs={{0,8},{1,9},{2,10},{3,11},{4,12},{5,13},{6,14},{7,15},{8,16},{9,17... | collective-permute-start | bytes 442376 | tf_op jit(solution)/shard_map/ppermute | solution.py:387
  171.0 7.4 %collective-permute-start.42 = (bf16[48,1536]{1,0:T(8,128)(2,1)S(1)}, bf16[48,1536]{1,0:T(8,128)(2,1)S(1)}, u32[]{:S(2)}, u32[]{:S(2)}) collective-permute-start(bf16[48,1536]{1,0:T(8,128)(2,1)S(1)} %get-tuple-element.111), channel_id=1, source_target_pairs={{0,24},{1,25},{2,26},{3,27},{4,28},{5,29},{6,30},{7,31},{8,0},{9,1... | collective-permute-start | bytes 442376 | tf_op jit(solution)/shard_map/ppermute | solution.py:387
  174.2 14.7 %collective-permute-start.41 = (bf16[48,1536]{1,0:T(8,128)(2,1)S(1)}, bf16[48,1536]{1,0:T(8,128)(2,1)S(1)}, u32[]{:S(2)}, u32[]{:S(2)}) collective-permute-start(bf16[48,1536]{1,0:T(8,128)(2,1)S(1)} %get-tuple-element.112), channel_id=1, source_target_pairs={{0,16},{1,17},{2,18},{3,19},{4,20},{5,21},{6,22},{7,23},{8,24},{9,... | collective-permute-start | bytes 442376 | tf_op jit(solution)/shard_map/ppermute | solution.py:387
  175.9 13.0 %collective-permute-start.40 = (bf16[48,1536]{1,0:T(8,128)(2,1)S(1)}, bf16[48,1536]{1,0:T(8,128)(2,1)S(1)}, u32[]{:S(2)}, u32[]{:S(2)}) collective-permute-start(bf16[48,1536]{1,0:T(8,128)(2,1)S(1)} %get-tuple-element.110), channel_id=1, source_target_pairs={{0,8},{1,9},{2,10},{3,11},{4,12},{5,13},{6,14},{7,15},{8,16},{9,17... | collective-permute-start | bytes 442376 | tf_op jit(solution)/shard_map/ppermute | solution.py:387
  175.9 22.7 %collective-permute-start.24 = (bf16[3,256,384]{2,1,0:T(8,128)(2,1)S(1)}, bf16[3,256,384]{2,1,0:T(8,128)(2,1)S(1)}, u32[]{:S(2)}, u32[]{:S(2)}) collective-permute-start(bf16[3,256,384]{2,1,0:T(8,128)(2,1)S(1)} %copy-done.30), channel_id=1, source_target_pairs={{0,1},{1,0},{2,3},{3,2},{4,5},{5,4},{6,7},{7,6},{8,9},{9,8},{10,11... | collective-permute-start | bytes 1769480 | tf_op jit(solution)/shard_map/ppermute | solution.py:387
  177.3 27.1 %copy-start.20 = (bf16[48,1536]{1,0:T(8,128)(2,1)}, bf16[48,1536]{1,0:T(8,128)(2,1)S(1)}, u32[]{:S(2)}) copy-start(bf16[48,1536]{1,0:T(8,128)(2,1)S(1)} %collective-permute-done.33.refs_5_) | copy-start | bytes 442372
  177.4 27.1 %collective-permute-start.25 = (bf16[3,256,384]{2,1,0:T(8,128)(2,1)S(1)}, bf16[3,256,384]{2,1,0:T(8,128)(2,1)S(1)}, u32[]{:S(2)}, u32[]{:S(2)}) collective-permute-start(bf16[3,256,384]{2,1,0:T(8,128)(2,1)S(1)} %copy-done.29), channel_id=1, source_target_pairs={{0,2},{1,3},{2,0},{3,1},{4,6},{5,7},{6,4},{7,5},{8,10},{9,11},{10,... | collective-permute-start | bytes 1769480 | tf_op jit(solution)/shard_map/ppermute | solution.py:387
  178.5 26.0 %collective-permute-start.26 = (bf16[3,256,384]{2,1,0:T(8,128)(2,1)S(1)}, bf16[3,256,384]{2,1,0:T(8,128)(2,1)S(1)}, u32[]{:S(2)}, u32[]{:S(2)}) collective-permute-start(bf16[3,256,384]{2,1,0:T(8,128)(2,1)S(1)} %copy-done.28), channel_id=1, source_target_pairs={{0,3},{1,2},{2,1},{3,0},{4,7},{5,6},{6,5},{7,4},{8,11},{9,10},{10,... | collective-permute-start | bytes 1769480 | tf_op jit(solution)/shard_map/ppermute | solution.py:387
  188.9 8.1 %collective-permute-start.34 = (bf16[48,1536]{1,0:T(8,128)(2,1)S(1)}, bf16[48,1536]{1,0:T(8,128)(2,1)S(1)}, u32[]{:S(2)}, u32[]{:S(2)}) collective-permute-start(bf16[48,1536]{1,0:T(8,128)(2,1)S(1)} %get-tuple-element.114), channel_id=1, source_target_pairs={{0,16},{1,17},{2,18},{3,19},{4,20},{5,21},{6,22},{7,23},{8,24},{9,... | collective-permute-start | bytes 442376 | tf_op jit(solution)/shard_map/ppermute | solution.py:387
  188.9 8.7 %collective-permute-start.35 = (bf16[48,1536]{1,0:T(8,128)(2,1)S(1)}, bf16[48,1536]{1,0:T(8,128)(2,1)S(1)}, u32[]{:S(2)}, u32[]{:S(2)}) collective-permute-start(bf16[48,1536]{1,0:T(8,128)(2,1)S(1)} %get-tuple-element.113), channel_id=1, source_target_pairs={{0,24},{1,25},{2,26},{3,27},{4,28},{5,29},{6,30},{7,31},{8,0},{9,1... | collective-permute-start | bytes 442376 | tf_op jit(solution)/shard_map/ppermute | solution.py:387
  191.6 17.9 %copy-start.10 = (bf16[48,1536]{1,0:T(8,128)(2,1)}, bf16[48,1536]{1,0:T(8,128)(2,1)S(1)}, u32[]{:S(2)}) copy-start(bf16[48,1536]{1,0:T(8,128)(2,1)S(1)} %add_convert_fusion.refs_0_) | copy-start | bytes 442372
  197.0 7.5 %copy-start.21 = (bf16[48,1536]{1,0:T(8,128)(2,1)}, bf16[48,1536]{1,0:T(8,128)(2,1)S(1)}, u32[]{:S(2)}) copy-start(bf16[48,1536]{1,0:T(8,128)(2,1)S(1)} %collective-permute-done.34.refs_6_) | copy-start | bytes 442372
  197.0 12.5 %collective-permute-start.43 = (bf16[48,1536]{1,0:T(8,128)(2,1)S(1)}, bf16[48,1536]{1,0:T(8,128)(2,1)S(1)}, u32[]{:S(2)}, u32[]{:S(2)}) collective-permute-start(bf16[48,1536]{1,0:T(8,128)(2,1)S(1)} %add_convert_fusion.refs_0_), channel_id=1, source_target_pairs={{0,1},{1,0},{2,3},{3,2},{4,5},{5,4},{6,7},{7,6},{8,9},{9,8},{10,11... | collective-permute-start | bytes 442376 | tf_op jit(solution)/shard_map/ppermute | solution.py:387
  197.5 6.9 %copy-start.22 = (bf16[48,1536]{1,0:T(8,128)(2,1)}, bf16[48,1536]{1,0:T(8,128)(2,1)S(1)}, u32[]{:S(2)}) copy-start(bf16[48,1536]{1,0:T(8,128)(2,1)S(1)} %collective-permute-done.35.refs_7_) | copy-start | bytes 442372
  197.5 12.0 %collective-permute-start.44 = (bf16[48,1536]{1,0:T(8,128)(2,1)S(1)}, bf16[48,1536]{1,0:T(8,128)(2,1)S(1)}, u32[]{:S(2)}, u32[]{:S(2)}) collective-permute-start(bf16[48,1536]{1,0:T(8,128)(2,1)S(1)} %add_convert_fusion.refs_0_), channel_id=1, source_target_pairs={{0,2},{1,3},{2,0},{3,1},{4,6},{5,7},{6,4},{7,5},{8,10},{9,11},{10,... | collective-permute-start | bytes 442376 | tf_op jit(solution)/shard_map/ppermute | solution.py:387
  198.6 10.9 %collective-permute-start.45 = (bf16[48,1536]{1,0:T(8,128)(2,1)S(1)}, bf16[48,1536]{1,0:T(8,128)(2,1)S(1)}, u32[]{:S(2)}, u32[]{:S(2)}) collective-permute-start(bf16[48,1536]{1,0:T(8,128)(2,1)S(1)} %add_convert_fusion.refs_0_), channel_id=1, source_target_pairs={{0,3},{1,2},{2,1},{3,0},{4,7},{5,6},{6,5},{7,4},{8,11},{9,10},{10,... | collective-permute-start | bytes 442376 | tf_op jit(solution)/shard_map/ppermute | solution.py:387
  (13 other events, 15.6 us)
